TPU v7x, 256 devices: a whole 4x4x8 slice. The times are simulated.
256 devices in a mesh: seq: 64 (over y, z, core), batch: 4 (over x).
Axes of the slice: x: 4, y: 4, z: 8, core: 2. Of those that a mesh axis runs over, the one named last changes fastest.
Arguments:
- inputs: bfloat16 [4, 16384, 1536], P('batch', 'seq'), may hold values from -6 to 6
- cotangent: bfloat16 [4, 16384, 1536], P('batch', 'seq'), may hold values from -6 to 6
- convolution_kernel: bfloat16 [3, 1536, 384], replicated, may hold values from -0.09375 to 0.09375
- mix_weight: bfloat16 [384, 1536], replicated, may hold values from -0.3125 to 0.3125
Outputs:
- outputs: bfloat16 [4, 16384, 1536], P('batch', 'seq')
- grad_inputs: bfloat16 [4, 16384, 1536], P('batch', 'seq')
- grad_conv: float32 [1769472], P(('seq', 'batch'))
All inputs are finite; a program needn't handle non-finite values.
Results may differ from a plain program's by a relative error of at most 0.0054.
Values may be sent and summed in bfloat16 or wider, within the bound.
No kernel may reach another device: no remote copies, remote signals or barrier semaphores. Data moves between devices by JAX's collectives and lax.ppermute only.
A program may use at most 128 MiB of HBM per device.

v0:
```python
import math

import jax
import jax.numpy as jnp
from jax import lax
from jax.sharding import PartitionSpec as P

DILATION_STEP = 16


def padded(cells, sides, width):
    for axis, dim in sides:
        count = lax.axis_size(axis)
        ends = count - 1
        head = lax.slice_in_dim(cells, 0, width, axis=dim)
        tail = lax.slice_in_dim(cells, cells.shape[dim] - width, cells.shape[dim], axis=dim)
        cells = jnp.concatenate(
            [
                lax.ppermute(tail, axis, [(i, (i + 1) % count) for i in range(ends)]),
                cells,
                lax.ppermute(head, axis, [((i + 1) % count, i) for i in range(ends)]),
            ],
            axis=dim,
        )
    return cells


def gelu_slope(values):
    return jax.vjp(jax.nn.gelu, values)[1](jnp.ones_like(values))[0]


def tap_contribution(rows, weight):
    return jnp.einsum("spc,ch->sph", rows, weight, preferred_element_type=jnp.float32)


def owner_sum(convolution_gradient):
    seq_count = lax.axis_size("seq")
    batch_count = lax.axis_size("batch")
    dev_count = seq_count * batch_count
    blocks = convolution_gradient.reshape(dev_count, -1)
    mine = lax.psum_scatter(blocks.reshape(-1), ("seq", "batch"), scatter_dimension=0, tiled=True)
    return (mine, dev_count)


def body(inputs, cotangent, convolution_kernel, mix_weight):
    seqs, position_count, channels = inputs.shape
    activated_values = jax.nn.gelu(inputs.astype(jnp.float32)).astype(jnp.bfloat16)
    padded_activation = padded(activated_values, (("seq", 1),), DILATION_STEP)
    preactivation = tap_contribution(padded_activation[:, 0:position_count], convolution_kernel[0])
    preactivation = preactivation + tap_contribution(
        padded_activation[:, DILATION_STEP : DILATION_STEP + position_count], convolution_kernel[1]
    )
    preactivation = preactivation + tap_contribution(
        padded_activation[:, 2 * DILATION_STEP : 2 * DILATION_STEP + position_count],
        convolution_kernel[2],
    )
    grad_hidden = jnp.einsum(
        "spc,hc->sph", cotangent, mix_weight, preferred_element_type=jnp.float32
    )
    preactivation_gradient = (grad_hidden * gelu_slope(preactivation)).astype(jnp.bfloat16)
    padded_gradient = padded(preactivation_gradient, (("seq", 1),), DILATION_STEP)
    hidden = jax.nn.gelu(preactivation).astype(jnp.bfloat16)
    mixed = jnp.einsum("sph,hc->spc", hidden, mix_weight, preferred_element_type=jnp.float32)
    outputs = (inputs.astype(jnp.float32) + mixed).astype(jnp.bfloat16)
    activation_gradient = jnp.einsum(
        "sph,ch->spc",
        padded_gradient[:, 2 * DILATION_STEP : 2 * DILATION_STEP + position_count],
        convolution_kernel[0],
        preferred_element_type=jnp.float32,
    )
    activation_gradient = activation_gradient + jnp.einsum(
        "sph,ch->spc",
        padded_gradient[:, DILATION_STEP : DILATION_STEP + position_count],
        convolution_kernel[1],
        preferred_element_type=jnp.float32,
    )
    activation_gradient = activation_gradient + jnp.einsum(
        "sph,ch->spc",
        padded_gradient[:, 0:position_count],
        convolution_kernel[2],
        preferred_element_type=jnp.float32,
    )
    grad_inputs = (
        cotangent.astype(jnp.float32) + activation_gradient * gelu_slope(inputs.astype(jnp.float32))
    ).astype(jnp.bfloat16)
    convolution_gradient = jnp.stack(
        [
            jnp.einsum(
                "spc,sph->ch",
                padded_activation[
                    :, tap_index * DILATION_STEP : tap_index * DILATION_STEP + position_count
                ],
                preactivation_gradient,
                preferred_element_type=jnp.float32,
            )
            for tap_index in range(3)
        ]
    )
    mine, dev_count = owner_sum(convolution_gradient)
    factor = 1.0 / math.sqrt(seqs * position_count * dev_count)
    grad_conv = mine * factor
    return (outputs, grad_inputs, grad_conv)


def solution(mesh):
    in_specs = (P("batch", "seq", None), P("batch", "seq", None), P(), P())
    out_specs = (P("batch", "seq", None), P("batch", "seq", None), P(("seq", "batch")))
    return jax.shard_map(body, mesh=mesh, in_specs=in_specs, out_specs=out_specs, check_vma=False)
```

profile of v0, /device:TPU:8, one launch (start us, length us, event | category | flops | bytes accessed | tf_op | source)
XLA Modules:
  0.0 320.2 jit_solution(9244255609060758145)
XLA Ops:
  7.2 0.0 all-reduce.3.cloned.1.call-start
  7.2 1.8 fusion.12
  9.1 7.1 %collective-permute-start.1 = (bf16[1,16,1536]{2,1,0:T(8,128)(2,1)S(1)}, bf16[1,16,1536]{2,1,0:T(8,128)(2,1)S(1)}, u32[]{:S(2)}, u32[]{:S(2)}) collective-permute-start(bf16[1,16,1536]{2,1,0:T(8,128)(2,1)S(1)} %get-tuple-element.4), channel_id=1, source_target_pairs={{4,0},{8,4},{12,8},{16,12},{20,16},{24,20},{28,24},{32,28},{36,32}... | collective-permute-start | bytes 147464 | tf_op jit(solution)/shard_map/ppermute | solution.py:21
  16.2 2.2 collective-permute-start
  18.4 2.0 fusion.21
  20.4 0.6 fusion.17
  21.0 3.0 collective-permute-done
  23.9 0.6 fusion.14
  24.5 0.7 fusion.25
  25.2 0.8 convolution_bitcast_fusion.1
  26.1 0.6 convolution_bitcast_fusion
  26.7 0.6 convolution_bitcast_fusion.2
  27.3 3.4 %pad_maximum_fusion = f32[3,1536,384]{2,1,0:T(8,128)} fusion(f32[1,1536,384]{2,1,0:T(8,128)S(1)} %convolution_bitcast_fusion, f32[1,1536,384]{2,1,0:T(8,128)S(1)} %convolution_bitcast_fusion.1, f32[1,1536,384]{2,1,0:T(8,128)S(1)} %convolution_bitcast_fusion.2), kind=kLoop, calls=%fused_computation | loop fusion | flops 3538944 | bytes 14155776 | tf_op jit(solution)/shard_map/stack | solution.py:86
  30.7 8.2 %reshape_reshape.3 = f32[1769472]{0:T(1024)} reshape(f32[3,1536,384]{2,1,0:T(8,128)} %pad_maximum_fusion) | data formatting | bytes 14155776 | tf_op jit(solution)/shard_map/reshape;reshape | solution.py:41
  38.9 0.0 all-reduce.3.cloned.1.call-update
  38.9 1.9 collective-permute-start.3
  40.9 1.5 fusion.5
  42.3 1.9 fusion.19
  44.2 5.8 %collective-permute-start.2 = (bf16[1,16,384]{2,1,0:T(8,128)(2,1)S(1)}, bf16[1,16,384]{2,1,0:T(8,128)(2,1)S(1)}, u32[]{:S(2)}, u32[]{:S(2)}) collective-permute-start(bf16[1,16,384]{2,1,0:T(8,128)(2,1)S(1)} %get-tuple-element.5), channel_id=1, source_target_pairs={{4,0},{8,4},{12,8},{16,12},{20,16},{24,20},{28,24},{32,28},{36,32}... | collective-permute-start | bytes 36872 | tf_op jit(solution)/shard_map/ppermute | solution.py:21
  50.0 0.6 fusion.15
  50.6 0.8 collective-permute-done.2
  51.3 2.4 fusion.4
  53.7 258.2 %all-reduce.3.cloned.1.call-done = f32[1769472]{0:T(1024)} async-done(((f32[1769472]{0:T(1024)}), f32[1769472]{0:T(1024)}) %all-reduce.3.cloned.1.call-update) | async-done | bytes 7077904
  311.9 1.4 dynamic-slice_multiply_fusion
  (14 shorter events, 0.1 us)
Async XLA Ops:
  7.2 17.4 %copy-start = (bf16[384,1536]{1,0:T(8,128)(2,1)S(1)}, bf16[384,1536]{1,0:T(8,128)(2,1)}, u32[]{:S(2)}) copy-start(bf16[384,1536]{1,0:T(8,128)(2,1)} %param.7) | copy-start | bytes 3538948
  7.2 11.2 %copy-start.1 = (bf16[1,256,1536]{2,1,0:T(8,128)(2,1)S(1)}, bf16[1,256,1536]{2,1,0:T(8,128)(2,1)}, u32[]{:S(2)}) copy-start(bf16[1,256,1536]{2,1,0:T(8,128)(2,1)} %param.4) | copy-start | bytes 2359300
  7.2 304.7 %all-reduce.3.cloned.1.call-start = ((), (), s32[]{:S(2)}) async-start(), calls=%async_computation | async-start | bytes 14155776
  9.1 11.3 %collective-permute-start.1 = (bf16[1,16,1536]{2,1,0:T(8,128)(2,1)S(1)}, bf16[1,16,1536]{2,1,0:T(8,128)(2,1)S(1)}, u32[]{:S(2)}, u32[]{:S(2)}) collective-permute-start(bf16[1,16,1536]{2,1,0:T(8,128)(2,1)S(1)} %get-tuple-element.4), channel_id=1, source_target_pairs={{4,0},{8,4},{12,8},{16,12},{20,16},{24,20},{28,24},{32,28},{36,32}... | collective-permute-start | bytes 147464 | tf_op jit(solution)/shard_map/ppermute | solution.py:21
  16.2 4.2 %copy-start.2 = (bf16[3,1536,384]{2,1,0:T(8,128)(2,1)S(1)}, bf16[3,1536,384]{2,1,0:T(8,128)(2,1)}, u32[]{:S(2)}) copy-start(bf16[3,1536,384]{2,1,0:T(8,128)(2,1)} %param.6) | copy-start | bytes 10616836
  16.2 7.8 %collective-permute-start = (bf16[1,16,1536]{2,1,0:T(8,128)(2,1)S(1)}, bf16[1,16,1536]{2,1,0:T(8,128)(2,1)S(1)}, u32[]{:S(2)}, u32[]{:S(2)}) collective-permute-start(bf16[1,16,1536]{2,1,0:T(8,128)(2,1)S(1)} %get-tuple-element.3), channel_id=1, source_target_pairs={{0,4},{4,8},{8,12},{12,16},{16,20},{20,24},{24,28},{28,32},{32,36}... | collective-permute-start | bytes 147464 | tf_op jit(solution)/shard_map/ppermute | solution.py:19
  21.0 3.6 %copy-start.4 = (bf16[1,256,1536]{2,1,0:T(8,128)(2,1)S(1)}, bf16[1,256,1536]{2,1,0:T(8,128)(2,1)}, u32[]{:S(2)}) copy-start(bf16[1,256,1536]{2,1,0:T(8,128)(2,1)} %param.5) | copy-start | bytes 2359300
  38.9 11.0 %collective-permute-start.3 = (bf16[1,16,384]{2,1,0:T(8,128)(2,1)S(1)}, bf16[1,16,384]{2,1,0:T(8,128)(2,1)S(1)}, u32[]{:S(2)}, u32[]{:S(2)}) collective-permute-start(bf16[1,16,384]{2,1,0:T(8,128)(2,1)S(1)} %get-tuple-element.6), channel_id=1, source_target_pairs={{0,4},{4,8},{8,12},{12,16},{16,20},{20,24},{24,28},{28,32},{32,36}... | collective-permute-start | bytes 36872 | tf_op jit(solution)/shard_map/ppermute | solution.py:19
  40.9 9.1 %copy-start.3 = (bf16[3,1536,384]{2,1,0:T(8,128)(2,1)S(1)}, bf16[3,1536,384]{2,1,0:T(8,128)(2,1)}, u32[]{:S(2)}) copy-start(bf16[3,1536,384]{2,1,0:T(8,128)(2,1)} %param.6) | copy-start | bytes 10616836
  44.2 7.1 %collective-permute-start.2 = (bf16[1,16,384]{2,1,0:T(8,128)(2,1)S(1)}, bf16[1,16,384]{2,1,0:T(8,128)(2,1)S(1)}, u32[]{:S(2)}, u32[]{:S(2)}) collective-permute-start(bf16[1,16,384]{2,1,0:T(8,128)(2,1)S(1)} %get-tuple-element.5), channel_id=1, source_target_pairs={{4,0},{8,4},{12,8},{16,12},{20,16},{24,20},{28,24},{32,28},{36,32}... | collective-permute-start | bytes 36872 | tf_op jit(solution)/shard_map/ppermute | solution.py:21
Sparse Core Ops, SparseCore 0:
  39.0 272.8 all-reduce.2
where the time goes:
time: 321 us; the launch traced here: 320 us
  waiting for transfers between devices  262 us (82%)
  starting transfers between devices  17 us (5%)
  between operations  14.2 us (4%)
  matrix products  12.2 us (4%)
  local copies, waits for them, and re-layouts  8.27 us (3%)
  other arithmetic  6.63 us (2%)
    unnamed x2, waiting for transfers between devices  258 us
    ppermute x2, starting transfers between devices, padded(): lax.ppermute(head, axis, [((i + 1) % count, i) for i in range(ends)])  12.8 us
    another operation x1, local copies, waits for them, and re-layouts, owner_sum(): blocks.reshape(-1)  8.23 us
  transfers between devices with their start and end apart: 5, of which 3 were waited for; matrix products, arithmetic and copies ran while one was open for 3% of the time, Pallas kernels for 0%

commit v1 on v0

v1 whole, which is shorter than its diff:
```python
import math

import jax
import jax.numpy as jnp
from jax import lax
from jax.sharding import PartitionSpec as P

DILATION_STEP = 16
Y, Z, CORES, X = 4, 8, 2, 4
HALF = 40


def seq_pairs(move):
    pairs = []
    for s in range(Y * Z * CORES):
        y, z, c = move(s // (Z * CORES), (s // CORES) % Z, s % CORES)
        pairs.append((s, (y * Z + z) * CORES + c))
    return pairs


def z_turn(z):
    return (z + 2 * (z % 2) - 1) % Z


def z_far(z):
    return (11 - 4 * (((z + 1) // 2) % 2) - z) % Z


def pick(blocks, *indices):
    return jnp.concatenate([lax.dynamic_slice_in_dim(blocks, i, 1, 0) for i in indices], 0)


def sent(values, axis, pairs, dtype=jnp.bfloat16):
    return lax.ppermute(values.astype(dtype), axis, pairs).astype(jnp.float32)


def neighbours(edge_tail, edge_head):
    count = lax.axis_size("seq")
    before = lax.ppermute(edge_tail, "seq", [(i, i + 1) for i in range(count - 1)])
    after = lax.ppermute(edge_head, "seq", [(i + 1, i) for i in range(count - 1)])
    return before, after


def gelu_slope(values):
    return jax.vjp(jax.nn.gelu, values)[1](jnp.ones_like(values))[0]


def y_rounds(blocks, y, first, second):
    one = seq_pairs(lambda y, z, c: (y ^ first, z, c))
    two = seq_pairs(lambda y, z, c: (y ^ second, z, c))
    kept = pick(blocks, y, y ^ second) + sent(
        pick(blocks, y ^ first, y ^ first ^ second), "seq", one
    )
    return kept[0] + sent(kept[1], "seq", two)


def owner_sum(gradient):
    s = lax.axis_index("seq")
    x = lax.axis_index("batch")
    y, z, c = s // (Z * CORES), (s // CORES) % Z, s % CORES
    rows = gradient.shape[0] // (Y * Z * CORES)
    cols = gradient.shape[1]
    blocks = gradient.reshape(Y * Z, CORES, rows, cols)
    other = lax.dynamic_index_in_dim(blocks, 1 - c, 1, keepdims=False)
    mine = lax.dynamic_index_in_dim(blocks, c, 1, keepdims=False)
    mine = mine + sent(other, "seq", seq_pairs(lambda y, z, c: (y, z, 1 - c)))
    mine = mine.reshape(Y, Z, rows, cols)
    part = jnp.concatenate(
        [y_rounds(mine[:, :, :HALF], y, 1, 3), y_rounds(mine[:, :, HALF:], y, 3, 1)], 1
    )
    near = z ^ 1
    part = pick(part, z, z_far(z), z_turn(z), z_far(z_turn(z))) + sent(
        pick(part, near, z_far(near), z_turn(near), z_far(z_turn(near))),
        "seq",
        seq_pairs(lambda y, z, c: (y, z ^ 1, c)),
    )
    part = part[:2] + sent(part[2:], "seq", seq_pairs(lambda y, z, c: (y, z_turn(z), c)))
    part = part[0] + sent(
        part[1], "seq", seq_pairs(lambda y, z, c: (y, z_far(z), c)), jnp.float32
    )
    part = part.reshape(X, rows // X, cols)
    part = pick(part, x, x ^ 3) + sent(
        pick(part, x ^ 1, x ^ 2), "batch", [(i, i ^ 1) for i in range(X)], jnp.float32
    )
    part = part[0] + sent(part[1], "batch", [(i, i ^ 3) for i in range(X)], jnp.float32)
    return part.reshape(-1)


def body(inputs, cotangent, convolution_kernel, mix_weight):
    seqs, position_count, channels = inputs.shape
    x = inputs[0]
    ct = cotangent[0]
    inner = mix_weight.shape[0]
    step = DILATION_STEP
    before, after = neighbours(x[-step:], x[:step])
    padded = jnp.concatenate([before, x, after], 0)
    activated = jax.nn.gelu(padded.astype(jnp.float32)).astype(jnp.bfloat16)
    taps = jnp.concatenate(
        [activated[k * step : k * step + position_count] for k in range(3)], 1
    )
    kernel_rows = convolution_kernel.reshape(3 * channels, inner)
    preact = jnp.dot(taps, kernel_rows, preferred_element_type=jnp.float32)
    grad_hidden = lax.dot_general(
        ct, mix_weight, (((1,), (1,)), ((), ())), preferred_element_type=jnp.float32
    )
    pre_grad = (grad_hidden * gelu_slope(preact)).astype(jnp.bfloat16)
    gradient = lax.dot_general(
        taps, pre_grad, (((0,), (0,)), ((), ())), preferred_element_type=jnp.float32
    )
    mine = owner_sum(gradient)
    factor = 1.0 / math.sqrt(seqs * position_count * lax.axis_size("seq") * lax.axis_size("batch"))
    grad_conv = mine * factor

    before, after = neighbours(pre_grad[-step:], pre_grad[:step])
    padded_grad = jnp.concatenate([before, pre_grad, after], 0)
    hidden = jax.nn.gelu(preact).astype(jnp.bfloat16)
    mixed = jnp.dot(hidden, mix_weight, preferred_element_type=jnp.float32)
    outputs = (x.astype(jnp.float32) + mixed).astype(jnp.bfloat16)
    act_grad = sum(
        lax.dot_general(
            padded_grad[(2 - k) * step : (2 - k) * step + position_count],
            convolution_kernel[k],
            (((1,), (1,)), ((), ())),
            preferred_element_type=jnp.float32,
        )
        for k in range(3)
    )
    grad_inputs = (
        ct.astype(jnp.float32) + act_grad * gelu_slope(x.astype(jnp.float32))
    ).astype(jnp.bfloat16)
    return outputs[None], grad_inputs[None], grad_conv


def solution(mesh):
    in_specs = (P("batch", "seq", None), P("batch", "seq", None), P(), P())
    out_specs = (P("batch", "seq", None), P("batch", "seq", None), P(("seq", "batch")))
    return jax.shard_map(body, mesh=mesh, in_specs=in_specs, out_specs=out_specs, check_vma=False)
```

time: 321 us -> 96 us (0.30)
  waiting for transfers between devices: 262 us -> 27.8 us
  starting transfers between devices: 17 us -> 36.9 us
  between operations: 14.2 us -> 1.41 us
    unnamed x2 -> x0, waiting for transfers between devices: 258 us -> none
    ppermute x4 -> x14, waiting for transfers between devices: 3.73 us -> 27.8 us  [the longest x10 26.1 us: sent(): return lax.ppermute(values.astype(dtype), axis, pairs).astype(jnp.float32)]
    ppermute x4 -> x14, starting transfers between devices: 16.9 us -> 36.9 us  [the longest x10 20.2 us: sent(): return lax.ppermute(values.astype(dtype), axis, pairs).astype(jnp.float32)]
    another operation x1 -> x2, local copies, waits for them, and re-layouts: 8.23 us -> 0.11 us  [owner_sum(): blocks.reshape(-1)]
    unnamed x10 -> x22, local copies, waits for them, and re-layouts: 0.03 us -> 5.46 us
    add x0 -> x9, other arithmetic: none -> 3.91 us  [the longest x1 2.84 us: owner_sum(): mine = mine + sent(other, 'seq', seq_pairs(lambda y, z, c: (y, z, 1 - c)))]
    another operation x1, other arithmetic: 3.38 us -> 0.04 us  [body(): jnp.stack([jnp.einsum('spc,sph->ch', padded_activation[:, tap_index * DIL...]
    dot_general x11 -> x7, matrix products: 12.2 us -> 12.5 us  [the longest x3 7.54 us: body(): lax.dot_general(padded_grad[(2 - k) * step:(2 - k) * step + position_coun...]
  transfers between devices with their start and end apart: 5 -> 14, of which waited for: 3 -> 9; matrix products, arithmetic and copies ran while one was open for 3% -> 14% of each run, Pallas kernels for 0% -> 0%
where the time goes in v1:
time: 96 us; the launch traced here: 95.5 us
  starting transfers between devices  36.9 us (38%)
  waiting for transfers between devices  27.8 us (29%)
  matrix products  12.5 us (13%)
  local copies, waits for them, and re-layouts  11 us (11%)
  other arithmetic  5.9 us (6%)
  between operations  1.41 us (1%)
    ppermute x10, waiting for transfers between devices, sent(): return lax.ppermute(values.astype(dtype), axis, pairs).astype(jnp.float32)  26.1 us
    ppermute x10, starting transfers between devices, sent(): return lax.ppermute(values.astype(dtype), axis, pairs).astype(jnp.float32)  20.2 us
    ppermute x2, starting transfers between devices, neighbours(): lax.ppermute(edge_head, 'seq', [(i + 1, i) for i in range(count - 1)])  12.8 us
    dot_general x3, matrix products, body(): lax.dot_general(padded_grad[(2 - k) * step:(2 - k) * step + position_coun...  7.54 us
    unnamed x22, local copies, waits for them, and re-layouts  5.46 us
    ppermute x2, starting transfers between devices, neighbours(): lax.ppermute(edge_tail, 'seq', [(i, i + 1) for i in range(count - 1)])  3.82 us
    add x1, other arithmetic, owner_sum(): mine = mine + sent(other, 'seq', seq_pairs(lambda y, z, c: (y, z, 1 - c)))  2.84 us
  transfers between devices with their start and end apart: 14, of which 9 were waited for; matrix products, arithmetic and copies ran while one was open for 14% of the time, Pallas kernels for 0%

profile of v1, /device:TPU:8, one launch (start us, length us, event | category | flops | bytes accessed | tf_op | source)
XLA Modules:
  0.0 95.5 jit_solution(1628118382274694604)
XLA Ops:
  1.6 1.9 %collective-permute-start = (bf16[16,1536]{1,0:T(8,128)(2,1)S(1)}, bf16[16,1536]{1,0:T(8,128)(2,1)S(1)}, u32[]{:S(2)}, u32[]{:S(2)}) collective-permute-start(bf16[16,1536]{1,0:T(8,128)(2,1)S(1)} %get-tuple-element.22), channel_id=1, source_target_pairs={{0,4},{4,8},{8,12},{12,16},{16,20},{20,24},{24,28},{28,32},{32,36}... | collective-permute-start | bytes 147464 | tf_op jit(solution)/shard_map/ppermute | solution.py:39
  3.5 7.1 %collective-permute-start.1 = (bf16[16,1536]{1,0:T(8,128)(2,1)S(1)}, bf16[16,1536]{1,0:T(8,128)(2,1)S(1)}, u32[]{:S(2)}, u32[]{:S(2)}) collective-permute-start(bf16[16,1536]{1,0:T(8,128)(2,1)S(1)} %get-tuple-element.23), channel_id=1, source_target_pairs={{4,0},{8,4},{12,8},{16,12},{20,16},{24,20},{28,24},{32,28},{36,32}... | collective-permute-start | bytes 147464 | tf_op jit(solution)/shard_map/ppermute | solution.py:40
  12.3 1.7 %fusion.13 = bf16[288,1536]{1,0:T(8,128)(2,1)S(1)} fusion(bf16[16,1536]{1,0:T(8,128)(2,1)S(1)} %collective-permute-done.1, bf16[256,1536]{1,0:T(8,128)(2,1)} %bitcast.66, bf16[16,1536]{1,0:T(8,128)(2,1)S(1)} %collective-permute-done), kind=kLoop, calls=%fused_computation.42 | loop fusion | flops 6635520 | bytes 1769472 | tf_op jit(solution)/shard_map/convert_element_type | solution.py:97
  14.3 1.8 %copy-done.3 = bf16[3,1536,384]{2,1,0:T(8,128)(2,1)S(1)} copy-done((bf16[3,1536,384]{2,1,0:T(8,128)(2,1)S(1)}, bf16[3,1536,384]{2,1,0:T(8,128)(2,1)}, u32[]{:S(2)}) %copy-start.3) | copy-done | bytes 3538968
  20.4 2.9 %copy-done.1 = f32[4608,384]{1,0:T(8,128)} copy-done((f32[4608,384]{1,0:T(8,128)}, f32[4608,384]{1,0:T(8,128)S(1)}, u32[]{:S(2)}) %copy-start.1) | copy-done | bytes 7077912
  23.9 3.4 %collective-permute-done.4 = bf16[32,72,384]{2,1,0:T(8,128)(2,1)} collective-permute-done((bf16[32,72,384]{2,1,0:T(8,128)(2,1)S(1)}, bf16[32,72,384]{2,1,0:T(8,128)(2,1)}, u32[]{:S(2)}, u32[]{:S(2)}) %collective-permute-start.4) | collective-permute-done | bytes 1769504 | tf_op jit(solution)/shard_map/ppermute | solution.py:34
  27.4 2.8 %bitcast_add_fusion = f32[32,72,384]{2,1,0:T(8,128)S(1)} fusion(bf16[32,72,384]{2,1,0:T(8,128)(2,1)} %collective-permute-done.4, f32[32,2,72,384]{3,2,1,0:T(8,128)} %bitcast.65, s32[]{:T(128)S(6)} %select_n.148), kind=kLoop, calls=%fused_computation | loop fusion | flops 1769472 | bytes 8847364 | tf_op jit(solution)/shard_map/add | solution.py:66
  32.4 2.3 %collective-permute-start.5 = (bf16[2,8,40,384]{3,2,1,0:T(8,128)(2,1)S(1)}, bf16[2,8,40,384]{3,2,1,0:T(8,128)(2,1)S(1)}, u32[]{:S(2)}, u32[]{:S(2)}) collective-permute-start(bf16[2,8,40,384]{3,2,1,0:T(8,128)(2,1)S(1)} %pad_maximum_fusion.3), channel_id=1, source_target_pairs={{0,64},{4,68},{8,72},{12,76},{16,80},{20,84},{24,88},{28,92},{32,9... | collective-permute-start | bytes 1474568 | tf_op jit(solution)/shard_map/ppermute | solution.py:34
  34.8 7.0 %collective-permute-done.7 = bf16[2,8,32,384]{3,2,1,0:T(8,128)(2,1)S(1)} collective-permute-done((bf16[2,8,32,384]{3,2,1,0:T(8,128)(2,1)S(1)}, bf16[2,8,32,384]{3,2,1,0:T(8,128)(2,1)S(1)}, u32[]{:S(2)}, u32[]{:S(2)}) %collective-permute-start.7) | collective-permute-done | bytes 393248 | tf_op jit(solution)/shard_map/ppermute | solution.py:34
  42.0 2.1 %collective-permute-start.8 = (bf16[8,32,384]{2,1,0:T(8,128)(2,1)S(1)}, bf16[8,32,384]{2,1,0:T(8,128)(2,1)S(1)}, u32[]{:S(2)}, u32[]{:S(2)}) collective-permute-start(bf16[8,32,384]{2,1,0:T(8,128)(2,1)S(1)} %fusion.42), channel_id=1, source_target_pairs={{0,64},{4,68},{8,72},{12,76},{16,80},{20,84},{24,88},{28,92},{32,9... | collective-permute-start | bytes 589832 | tf_op jit(solution)/shard_map/ppermute | solution.py:34
  44.1 2.6 %collective-permute-done.5 = bf16[2,8,40,384]{3,2,1,0:T(8,128)(2,1)S(1)} collective-permute-done((bf16[2,8,40,384]{3,2,1,0:T(8,128)(2,1)S(1)}, bf16[2,8,40,384]{3,2,1,0:T(8,128)(2,1)S(1)}, u32[]{:S(2)}, u32[]{:S(2)}) %collective-permute-start.5) | collective-permute-done | bytes 491552 | tf_op jit(solution)/shard_map/ppermute | solution.py:34
  47.0 3.1 %collective-permute-done.8 = bf16[8,32,384]{2,1,0:T(8,128)(2,1)S(1)} collective-permute-done((bf16[8,32,384]{2,1,0:T(8,128)(2,1)S(1)}, bf16[8,32,384]{2,1,0:T(8,128)(2,1)S(1)}, u32[]{:S(2)}, u32[]{:S(2)}) %collective-permute-start.8) | collective-permute-done | bytes 196640 | tf_op jit(solution)/shard_map/ppermute | solution.py:34
  50.2 3.2 %collective-permute-done.6 = bf16[8,40,384]{2,1,0:T(8,128)(2,1)S(1)} collective-permute-done((bf16[8,40,384]{2,1,0:T(8,128)(2,1)S(1)}, bf16[8,40,384]{2,1,0:T(8,128)(2,1)S(1)}, u32[]{:S(2)}, u32[]{:S(2)}) %collective-permute-start.6) | collective-permute-done | bytes 245792 | tf_op jit(solution)/shard_map/ppermute | solution.py:34
  53.8 1.9 %fusion.23 = f32[256,1536]{1,0:T(8,128)S(1)} fusion(bf16[256,384]{1,0:T(8,128)(2,1)S(1)} %copy-done.5, bf16[3,1536,384]{2,1,0:T(8,128)(2,1)} %param.6), kind=kOutput, calls=%fused_computation.53 | convolution fusion | flops 301989888 | bytes 2949120 | tf_op jit(solution)/shard_map/dot_general | solution.py:120
  55.7 3.8 %collective-permute-done.9 = bf16[4,72,384]{2,1,0:T(8,128)(2,1)S(1)} collective-permute-done((bf16[4,72,384]{2,1,0:T(8,128)(2,1)S(1)}, bf16[4,72,384]{2,1,0:T(8,128)(2,1)S(1)}, u32[]{:S(2)}, u32[]{:S(2)}) %collective-permute-start.9) | collective-permute-done | bytes 221216 | tf_op jit(solution)/shard_map/ppermute | solution.py:34
  59.6 3.8 %collective-permute-start.10 = (bf16[2,72,384]{2,1,0:T(8,128)(2,1)S(1)}, bf16[2,72,384]{2,1,0:T(8,128)(2,1)S(1)}, u32[]{:S(2)}, u32[]{:S(2)}) collective-permute-start(bf16[2,72,384]{2,1,0:T(8,128)(2,1)S(1)} %slice.164), channel_id=1, source_target_pairs={{0,56},{4,60},{8,16},{12,20},{16,8},{20,12},{24,32},{28,36},{32,24... | collective-permute-start | bytes 331784 | tf_op jit(solution)/shard_map/ppermute | solution.py:34
  64.9 2.0 %collective-permute-done.10 = bf16[2,72,384]{2,1,0:T(8,128)(2,1)S(1)} collective-permute-done((bf16[2,72,384]{2,1,0:T(8,128)(2,1)S(1)}, bf16[2,72,384]{2,1,0:T(8,128)(2,1)S(1)}, u32[]{:S(2)}, u32[]{:S(2)}) %collective-permute-start.10) | collective-permute-done | bytes 110624 | tf_op jit(solution)/shard_map/ppermute | solution.py:34
  67.0 5.3 %collective-permute-start.11 = (f32[72,384]{1,0:T(8,128)S(1)}, f32[72,384]{1,0:T(8,128)S(1)}, u32[]{:S(2)}, u32[]{:S(2)}) collective-permute-start(f32[72,384]{1,0:T(8,128)S(1)} %slice_bitcast_fusion.2), channel_id=1, source_target_pairs={{0,24},{4,28},{8,48},{12,52},{16,40},{20,44},{24,0},{28,4},{32,56}... | collective-permute-start | bytes 331784 | tf_op jit(solution)/shard_map/ppermute | solution.py:34
  72.9 1.9 %collective-permute-start.3 = (bf16[16,384]{1,0:T(8,128)(2,1)}, bf16[16,384]{1,0:T(8,128)(2,1)S(1)}, u32[]{:S(2)}, u32[]{:S(2)}) collective-permute-start(bf16[16,384]{1,0:T(8,128)(2,1)} %get-tuple-element.25), channel_id=1, source_target_pairs={{0,4},{4,8},{8,12},{12,16},{16,20},{20,24},{24,28},{28,32},{32,36}... | collective-permute-start | bytes 36872 | tf_op jit(solution)/shard_map/ppermute | solution.py:39
  74.8 5.8 %collective-permute-start.2 = (bf16[16,384]{1,0:T(8,128)(2,1)}, bf16[16,384]{1,0:T(8,128)(2,1)}, u32[]{:S(2)}, u32[]{:S(2)}) collective-permute-start(bf16[16,384]{1,0:T(8,128)(2,1)} %get-tuple-element.24), channel_id=1, source_target_pairs={{4,0},{8,4},{12,8},{16,12},{20,16},{24,20},{28,24},{32,28},{36,32}... | collective-permute-start | bytes 36872 | tf_op jit(solution)/shard_map/ppermute | solution.py:40
  83.7 1.7 %collective-permute-start.12 = (f32[2,18,384]{2,1,0:T(8,128)S(1)}, f32[2,18,384]{2,1,0:T(8,128)S(1)}, u32[]{:S(2)}, u32[]{:S(2)}) collective-permute-start(f32[2,18,384]{2,1,0:T(8,128)S(1)} %pad_maximum_fusion.10), channel_id=1, source_target_pairs={{0,1},{1,0},{2,3},{3,2},{4,5},{5,4},{6,7},{7,6},{8,9},{9,8},{10,11... | collective-permute-start | bytes 165896 | tf_op jit(solution)/shard_map/ppermute | solution.py:34
  85.5 2.0 %fusion.21 = f32[256,1536]{1,0:T(8,128)S(1)} fusion(bf16[3,1536,384]{2,1,0:T(8,128)(2,1)} %param.6, bf16[256,384]{1,0:T(8,128)(2,1)} %copy-done.4, bf16[16,384]{1,0:T(8,128)(2,1)S(1)} %collective-permute-done.3), kind=kOutput, calls=%fused_computation.51 | convolution fusion | flops 302383104 | bytes 2961408 | tf_op jit(solution)/shard_map/dot_general | solution.py:120
  88.3 2.8 %collective-permute-start.13 = (f32[18,384]{1,0:T(8,128)S(1)}, f32[18,384]{1,0:T(8,128)S(1)}, u32[]{:S(2)}, u32[]{:S(2)}) collective-permute-start(f32[18,384]{1,0:T(8,128)S(1)} %slice_bitcast_fusion.6), channel_id=1, source_target_pairs={{0,3},{1,2},{2,1},{3,0},{4,7},{5,6},{6,5},{7,4},{8,11},{9,10},{10,... | collective-permute-start | bytes 82952 | tf_op jit(solution)/shard_map/ppermute | solution.py:34
  91.2 3.7 %fusion.6 = bf16[1,256,1536]{2,1,0:T(8,128)(2,1)} fusion(f32[256,1536]{1,0:T(8,128)S(1)} %fusion.21, f32[256,1536]{1,0:T(8,128)S(1)} %fusion.23, bf16[3,1536,384]{2,1,0:T(8,128)(2,1)} %param.6, bf16[1,256,1536]{2,1,0:T(8,128)(2,1)S(1)} %copy-done.10, bf16[16,384]{1,0:T(8,128)(2,1)} %collective-permute-done.2, bf16[256,384]{1,0:T(8,128)(2,1)S(1)} %copy-done.6, ...), kind=kOutput, calls=%fused_computation.18 | convolution fusion | flops 311820288 | bytes 6893568 | tf_op jit(solution)/shard_map/dot_general | solution.py:120
  (68 shorter events, 17.4 us)
Async XLA Ops:
  0.6 17.6 %copy-start = (bf16[384,1536]{1,0:T(8,128)(2,1)S(1)}, bf16[384,1536]{1,0:T(8,128)(2,1)}, u32[]{:S(2)}) copy-start(bf16[384,1536]{1,0:T(8,128)(2,1)} %param.7) | copy-start | bytes 3538948
  1.6 9.0 %collective-permute-start = (bf16[16,1536]{1,0:T(8,128)(2,1)S(1)}, bf16[16,1536]{1,0:T(8,128)(2,1)S(1)}, u32[]{:S(2)}, u32[]{:S(2)}) collective-permute-start(bf16[16,1536]{1,0:T(8,128)(2,1)S(1)} %get-tuple-element.22), channel_id=1, source_target_pairs={{0,4},{4,8},{8,12},{12,16},{16,20},{20,24},{24,28},{28,32},{32,36}... | collective-permute-start | bytes 147464 | tf_op jit(solution)/shard_map/ppermute | solution.py:39
  3.5 8.8 %collective-permute-start.1 = (bf16[16,1536]{1,0:T(8,128)(2,1)S(1)}, bf16[16,1536]{1,0:T(8,128)(2,1)S(1)}, u32[]{:S(2)}, u32[]{:S(2)}) collective-permute-start(bf16[16,1536]{1,0:T(8,128)(2,1)S(1)} %get-tuple-element.23), channel_id=1, source_target_pairs={{4,0},{8,4},{12,8},{16,12},{20,16},{24,20},{28,24},{32,28},{36,32}... | collective-permute-start | bytes 147464 | tf_op jit(solution)/shard_map/ppermute | solution.py:40
  14.1 2.0 %copy-start.3 = (bf16[3,1536,384]{2,1,0:T(8,128)(2,1)S(1)}, bf16[3,1536,384]{2,1,0:T(8,128)(2,1)}, u32[]{:S(2)}) copy-start(bf16[3,1536,384]{2,1,0:T(8,128)(2,1)} %param.6) | copy-start | bytes 10616836
  16.1 2.2 %copy-start.9 = (bf16[1,256,1536]{2,1,0:T(8,128)(2,1)S(1)}, bf16[1,256,1536]{2,1,0:T(8,128)(2,1)}, u32[]{:S(2)}) copy-start(bf16[1,256,1536]{2,1,0:T(8,128)(2,1)} %param.5) | copy-start | bytes 2359300
  18.9 1.4 %copy-start.4 = (bf16[256,384]{1,0:T(8,128)(2,1)}, bf16[256,384]{1,0:T(8,128)(2,1)S(1)}, u32[]{:S(2)}) copy-start(bf16[256,384]{1,0:T(8,128)(2,1)S(1)} %fusion.29) | copy-start | bytes 589828
  20.4 2.9 %copy-start.1 = (f32[4608,384]{1,0:T(8,128)}, f32[4608,384]{1,0:T(8,128)S(1)}, u32[]{:S(2)}) copy-start(f32[4608,384]{1,0:T(8,128)S(1)} %fusion.30) | copy-start | bytes 21233668
  23.4 3.9 %collective-permute-start.4 = (bf16[32,72,384]{2,1,0:T(8,128)(2,1)S(1)}, bf16[32,72,384]{2,1,0:T(8,128)(2,1)}, u32[]{:S(2)}, u32[]{:S(2)}) collective-permute-start(bf16[32,72,384]{2,1,0:T(8,128)(2,1)S(1)} %fusion.14), channel_id=1, source_target_pairs={{0,4},{4,0},{8,12},{12,8},{16,20},{20,16},{24,28},{28,24},{32,36},... | collective-permute-start | bytes 5308424 | tf_op jit(solution)/shard_map/ppermute | solution.py:34
  30.6 11.2 %collective-permute-start.7 = (bf16[2,8,32,384]{3,2,1,0:T(8,128)(2,1)S(1)}, bf16[2,8,32,384]{3,2,1,0:T(8,128)(2,1)S(1)}, u32[]{:S(2)}, u32[]{:S(2)}) collective-permute-start(bf16[2,8,32,384]{3,2,1,0:T(8,128)(2,1)S(1)} %pad_maximum_fusion.4), channel_id=1, source_target_pairs={{0,192},{4,196},{8,200},{12,204},{16,208},{20,212},{24,216},{28,22... | collective-permute-start | bytes 1179656 | tf_op jit(solution)/shard_map/ppermute | solution.py:34
  32.4 14.3 %collective-permute-start.5 = (bf16[2,8,40,384]{3,2,1,0:T(8,128)(2,1)S(1)}, bf16[2,8,40,384]{3,2,1,0:T(8,128)(2,1)S(1)}, u32[]{:S(2)}, u32[]{:S(2)}) collective-permute-start(bf16[2,8,40,384]{3,2,1,0:T(8,128)(2,1)S(1)} %pad_maximum_fusion.3), channel_id=1, source_target_pairs={{0,64},{4,68},{8,72},{12,76},{16,80},{20,84},{24,88},{28,92},{32,9... | collective-permute-start | bytes 1474568 | tf_op jit(solution)/shard_map/ppermute | solution.py:34
  42.0 8.1 %collective-permute-start.8 = (bf16[8,32,384]{2,1,0:T(8,128)(2,1)S(1)}, bf16[8,32,384]{2,1,0:T(8,128)(2,1)S(1)}, u32[]{:S(2)}, u32[]{:S(2)}) collective-permute-start(bf16[8,32,384]{2,1,0:T(8,128)(2,1)S(1)} %fusion.42), channel_id=1, source_target_pairs={{0,64},{4,68},{8,72},{12,76},{16,80},{20,84},{24,88},{28,92},{32,9... | collective-permute-start | bytes 589832 | tf_op jit(solution)/shard_map/ppermute | solution.py:34
  46.9 6.9 %copy-start.5 = (bf16[256,384]{1,0:T(8,128)(2,1)S(1)}, bf16[256,384]{1,0:T(8,128)(2,1)}, u32[]{:S(2)}) copy-start(bf16[256,384]{1,0:T(8,128)(2,1)} %copy-done.4) | copy-start | bytes 589828
  46.9 6.5 %collective-permute-start.6 = (bf16[8,40,384]{2,1,0:T(8,128)(2,1)S(1)}, bf16[8,40,384]{2,1,0:T(8,128)(2,1)S(1)}, u32[]{:S(2)}, u32[]{:S(2)}) collective-permute-start(bf16[8,40,384]{2,1,0:T(8,128)(2,1)S(1)} %fusion.41), channel_id=1, source_target_pairs={{0,192},{4,196},{8,200},{12,204},{16,208},{20,212},{24,216},{28,22... | collective-permute-start | bytes 737288 | tf_op jit(solution)/shard_map/ppermute | solution.py:34
  53.5 6.0 %collective-permute-start.9 = (bf16[4,72,384]{2,1,0:T(8,128)(2,1)S(1)}, bf16[4,72,384]{2,1,0:T(8,128)(2,1)S(1)}, u32[]{:S(2)}, u32[]{:S(2)}) collective-permute-start(bf16[4,72,384]{2,1,0:T(8,128)(2,1)S(1)} %pad_maximum_fusion.5), channel_id=1, source_target_pairs={{0,8},{4,12},{8,0},{12,4},{16,24},{20,28},{24,16},{28,20},{32,40},... | collective-permute-start | bytes 663560 | tf_op jit(solution)/shard_map/ppermute | solution.py:34
  55.7 7.8 %copy-start.2 = (bf16[1,256,1536]{2,1,0:T(8,128)(2,1)S(1)}, bf16[1,256,1536]{2,1,0:T(8,128)(2,1)}, u32[]{:S(2)}) copy-start(bf16[1,256,1536]{2,1,0:T(8,128)(2,1)} %param.4) | copy-start | bytes 2359300
  55.7 7.8 %copy-start.8 = (f32[256,384]{1,0:T(8,128)S(1)}, f32[256,384]{1,0:T(8,128)}, u32[]{:S(2)}) copy-start(f32[256,384]{1,0:T(8,128)} %copy-done.7) | copy-start | bytes 1179652
  59.6 7.3 %collective-permute-start.10 = (bf16[2,72,384]{2,1,0:T(8,128)(2,1)S(1)}, bf16[2,72,384]{2,1,0:T(8,128)(2,1)S(1)}, u32[]{:S(2)}, u32[]{:S(2)}) collective-permute-start(bf16[2,72,384]{2,1,0:T(8,128)(2,1)S(1)} %slice.164), channel_id=1, source_target_pairs={{0,56},{4,60},{8,16},{12,20},{16,8},{20,12},{24,32},{28,36},{32,24... | collective-permute-start | bytes 331784 | tf_op jit(solution)/shard_map/ppermute | solution.py:34
  67.0 13.6 %collective-permute-start.11 = (f32[72,384]{1,0:T(8,128)S(1)}, f32[72,384]{1,0:T(8,128)S(1)}, u32[]{:S(2)}, u32[]{:S(2)}) collective-permute-start(f32[72,384]{1,0:T(8,128)S(1)} %slice_bitcast_fusion.2), channel_id=1, source_target_pairs={{0,24},{4,28},{8,48},{12,52},{16,40},{20,44},{24,0},{28,4},{32,56}... | collective-permute-start | bytes 331784 | tf_op jit(solution)/shard_map/ppermute | solution.py:34
  72.9 12.5 %collective-permute-start.3 = (bf16[16,384]{1,0:T(8,128)(2,1)}, bf16[16,384]{1,0:T(8,128)(2,1)S(1)}, u32[]{:S(2)}, u32[]{:S(2)}) collective-permute-start(bf16[16,384]{1,0:T(8,128)(2,1)} %get-tuple-element.25), channel_id=1, source_target_pairs={{0,4},{4,8},{8,12},{12,16},{16,20},{20,24},{24,28},{28,32},{32,36}... | collective-permute-start | bytes 36872 | tf_op jit(solution)/shard_map/ppermute | solution.py:39
  74.8 16.4 %collective-permute-start.2 = (bf16[16,384]{1,0:T(8,128)(2,1)}, bf16[16,384]{1,0:T(8,128)(2,1)}, u32[]{:S(2)}, u32[]{:S(2)}) collective-permute-start(bf16[16,384]{1,0:T(8,128)(2,1)} %get-tuple-element.24), channel_id=1, source_target_pairs={{4,0},{8,4},{12,8},{16,12},{20,16},{24,20},{28,24},{32,28},{36,32}... | collective-permute-start | bytes 36872 | tf_op jit(solution)/shard_map/ppermute | solution.py:40
  83.7 7.5 %copy-start.6 = (bf16[256,384]{1,0:T(8,128)(2,1)S(1)}, bf16[256,384]{1,0:T(8,128)(2,1)}, u32[]{:S(2)}) copy-start(bf16[256,384]{1,0:T(8,128)(2,1)} %copy-done.4) | copy-start | bytes 589828
  83.7 7.5 %copy-start.10 = (bf16[1,256,1536]{2,1,0:T(8,128)(2,1)S(1)}, bf16[1,256,1536]{2,1,0:T(8,128)(2,1)}, u32[]{:S(2)}) copy-start(bf16[1,256,1536]{2,1,0:T(8,128)(2,1)} %param.5) | copy-start | bytes 2359300
  83.7 4.6 %collective-permute-start.12 = (f32[2,18,384]{2,1,0:T(8,128)S(1)}, f32[2,18,384]{2,1,0:T(8,128)S(1)}, u32[]{:S(2)}, u32[]{:S(2)}) collective-permute-start(f32[2,18,384]{2,1,0:T(8,128)S(1)} %pad_maximum_fusion.10), channel_id=1, source_target_pairs={{0,1},{1,0},{2,3},{3,2},{4,5},{5,4},{6,7},{7,6},{8,9},{9,8},{10,11... | collective-permute-start | bytes 165896 | tf_op jit(solution)/shard_map/ppermute | solution.py:34
  88.3 6.6 %collective-permute-start.13 = (f32[18,384]{1,0:T(8,128)S(1)}, f32[18,384]{1,0:T(8,128)S(1)}, u32[]{:S(2)}, u32[]{:S(2)}) collective-permute-start(f32[18,384]{1,0:T(8,128)S(1)} %slice_bitcast_fusion.6), channel_id=1, source_target_pairs={{0,3},{1,2},{2,1},{3,0},{4,7},{5,6},{6,5},{7,4},{8,11},{9,10},{10,... | collective-permute-start | bytes 82952 | tf_op jit(solution)/shard_map/ppermute | solution.py:34
  (1 other events, 0.7 us)

commit v2 on v1

v2 whole, which is shorter than its diff:
```python
import math

import jax
import jax.numpy as jnp
from jax import lax
from jax.experimental import pallas as pl
from jax.experimental.pallas import tpu as pltpu
from jax.sharding import Mesh, PartitionSpec as P

DILATION_STEP = 16
Y, Z, CORES, X = 4, 8, 2, 4
SEQ = ("y", "z", "core")


def neighbours(tail, head):
    count = Y * Z * CORES
    before = lax.ppermute(tail, SEQ, [(i, i + 1) for i in range(count - 1)])
    after = lax.ppermute(head, SEQ, [(i + 1, i) for i in range(count - 1)])
    return before, after


def swap_cores(values):
    return lax.ppermute(values, "core", [(0, 1), (1, 0)])


def gelu(values):
    return jax.nn.gelu(values.astype(jnp.float32)).astype(jnp.bfloat16)


def gelu_slope(values):
    return jax.vjp(jax.nn.gelu, values)[1](jnp.ones_like(values))[0]


def shifted(padded, count):
    return jnp.concatenate(
        [padded[k * DILATION_STEP : k * DILATION_STEP + count] for k in range(3)], 1
    )


def owned_rows(rows, core):
    shape = (X * Z * rows, Z * CORES * X * rows)
    target = lax.broadcasted_iota(jnp.int32, shape, 0)
    source = lax.broadcasted_iota(jnp.int32, shape, 1)
    x, z, i = target // (Z * rows), (target // rows) % Z, target % rows
    return (source == ((z * CORES + core) * X + x) * rows + i).astype(jnp.bfloat16)


def gradient_kernel(act_a, act_b, grad_a, grad_b, select, out):
    count, inner = grad_a.shape
    channels = act_a.shape[1]
    chunk = 384
    per_y = 3 * channels // Y // chunk
    left_a, left_b = grad_a[...].T, grad_b[...].T
    for y in range(Y):
        parts = []
        for j in range(y * per_y, (y + 1) * per_y):
            tap, ch = divmod(j * chunk, channels)
            rows = slice(tap * DILATION_STEP, tap * DILATION_STEP + count)
            part = jnp.dot(
                left_a, act_a[rows, ch : ch + chunk], preferred_element_type=jnp.float32
            ) + jnp.dot(left_b, act_b[rows, ch : ch + chunk], preferred_element_type=jnp.float32)
            parts.append(part.astype(jnp.bfloat16))
        block = lax.dot_general(
            select[...],
            jnp.concatenate(parts, 1),
            (((1,), (1,)), ((), ())),
            preferred_element_type=jnp.float32,
        ).astype(jnp.bfloat16)
        for x in range(X):
            size = block.shape[0] // X
            out[y * X + x] = block[x * size : (x + 1) * size]


def owner_sum(act_a, act_b, grad_a, grad_b):
    inner = grad_a.shape[1]
    rows = 3 * act_a.shape[1] // (Y * Z * CORES * X)
    select = owned_rows(rows, lax.axis_index("core"))
    ordered = pl.pallas_call(
        gradient_kernel,
        out_shape=jax.ShapeDtypeStruct((Y * X, Z * rows, inner), jnp.bfloat16),
        in_specs=[pl.BlockSpec(memory_space=pltpu.VMEM)] * 5,
        out_specs=pl.BlockSpec(memory_space=pltpu.VMEM),
        compiler_params=pltpu.CompilerParams(vmem_limit_bytes=24 << 20),
        cost_estimate=pl.CostEstimate(
            flops=4 * 10**9, bytes_accessed=6 * 10**6, transcendentals=0
        ),
    )(act_a, act_b, grad_a, grad_b, select)
    terms = lax.all_to_all(ordered, ("y", "x"), 0, 0, tiled=True)
    part = jnp.sum(terms.astype(jnp.float32), 0).astype(jnp.bfloat16)
    terms = lax.all_to_all(part.reshape(Z, rows, inner), "z", 0, 0, tiled=True)
    return jnp.sum(terms.astype(jnp.float32), 0).reshape(-1)


def body(inputs, cotangent, convolution_kernel, mix_weight):
    seqs, position_count, channels = inputs.shape
    x = inputs[0]
    ct = cotangent[0]
    inner = mix_weight.shape[0]
    step = DILATION_STEP
    before, after = neighbours(x[-step:], x[:step])
    activated = jnp.concatenate([gelu(before), gelu(x), gelu(after)], 0)
    activated_pair = swap_cores(activated)
    taps = shifted(activated, position_count)
    kernel_rows = convolution_kernel.reshape(3 * channels, inner)
    preact = jnp.dot(taps, kernel_rows, preferred_element_type=jnp.float32)
    grad_hidden = lax.dot_general(
        ct, mix_weight, (((1,), (1,)), ((), ())), preferred_element_type=jnp.float32
    )
    pre_grad = (grad_hidden * gelu_slope(preact)).astype(jnp.bfloat16)
    pre_grad_pair = swap_cores(pre_grad)
    mine = owner_sum(activated, activated_pair, pre_grad, pre_grad_pair)
    factor = 1.0 / math.sqrt(seqs * position_count * Y * Z * CORES * X)
    grad_conv = mine * factor

    before, after = neighbours(pre_grad[-step:], pre_grad[:step])
    padded_grad = jnp.concatenate([before, pre_grad, after], 0)
    hidden = gelu(preact)
    mixed = jnp.dot(hidden, mix_weight, preferred_element_type=jnp.float32)
    outputs = (x.astype(jnp.float32) + mixed).astype(jnp.bfloat16)
    act_grad = sum(
        lax.dot_general(
            padded_grad[(2 - k) * step : (2 - k) * step + position_count],
            convolution_kernel[k],
            (((1,), (1,)), ((), ())),
            preferred_element_type=jnp.float32,
        )
        for k in range(3)
    )
    grad_inputs = (
        ct.astype(jnp.float32) + act_grad * gelu_slope(x.astype(jnp.float32))
    ).astype(jnp.bfloat16)
    return outputs[None], grad_inputs[None], grad_conv


def solution(mesh):
    devices = mesh.devices.reshape(Y, Z, CORES, X)
    fine = Mesh(devices, ("y", "z", "core", "x"))
    rows = P("x", SEQ, None)
    return jax.shard_map(
        body,
        mesh=fine,
        in_specs=(rows, rows, P(), P()),
        out_specs=(rows, rows, P(("y", "z", "core", "x"))),
        check_vma=False,
    )
```

time: 96 us -> 78.5 us (0.82)
  waiting for transfers between devices: 27.8 us -> 16.8 us
  local copies, waits for them, and re-layouts: 11 us -> 2.26 us
  Pallas kernels: 0 us -> 6.77 us
  starting transfers between devices: 36.9 us -> 31.4 us
  matrix products: 12.5 us -> 16.7 us
  other arithmetic: 5.9 us -> 3.3 us
    ppermute x14 -> x6, waiting for transfers between devices: 27.8 us -> 1.04 us  [the longest x2 1.03 us: swap_cores(): return lax.ppermute(values, 'core', [(0, 1), (1, 0)])]
    ppermute x14 -> x6, starting transfers between devices: 36.9 us -> 17.4 us  [the longest x2 12.8 us: neighbours(): after = lax.ppermute(head, SEQ, [(i + 1, i) for i in range(count - 1)])]
    all_to_all x0 -> x2, waiting for transfers between devices: none -> 15.7 us  [the longest x1 11.5 us: owner_sum(): terms = lax.all_to_all(ordered, ('y', 'x'), 0, 0, tiled=True)]
    all_to_all x0 -> x2, starting transfers between devices: none -> 14.1 us  [the longest x1 7.5 us: owner_sum(): terms = lax.all_to_all(ordered, ('y', 'x'), 0, 0, tiled=True)]
    pallas_call x0 -> x1, Pallas kernels: none -> 6.77 us  [owner_sum(): pl.pallas_call(gradient_kernel, out_shape=jax.ShapeDtypeStruct((Y * X, Z...]
    unnamed x22 -> x6, local copies, waits for them, and re-layouts: 5.46 us -> 0.02 us
    add x9 -> x0, other arithmetic: 3.91 us -> none  [the longest x1 2.84 us: owner_sum(): mine = mine + sent(other, 'seq', seq_pairs(lambda y, z, c: (y, z, 1 - c)))]
    dot_general x3, matrix products: 7.54 us -> 11.1 us  [body(): lax.dot_general(padded_grad[(2 - k) * step:(2 - k) * step + position_coun...]
  transfers between devices with their start and end apart: 14 -> 8, of which waited for: 9 -> 3; matrix products, arithmetic and copies ran while one was open for 14% -> 21% of each run, Pallas kernels for 0% -> 0%
where the time goes in v2:
time: 78.5 us; the launch traced here: 78.1 us
  starting transfers between devices  31.4 us (40%)
  waiting for transfers between devices  16.8 us (21%)
  matrix products  16.7 us (21%)
  Pallas kernels  6.77 us (9%)
  other arithmetic  3.3 us (4%)
  local copies, waits for them, and re-layouts  2.26 us (3%)
  between operations  0.84 us (1%)
    ppermute x2, starting transfers between devices, neighbours(): after = lax.ppermute(head, SEQ, [(i + 1, i) for i in range(count - 1)])  12.8 us
    all_to_all x1, waiting for transfers between devices, owner_sum(): terms = lax.all_to_all(ordered, ('y', 'x'), 0, 0, tiled=True)  11.5 us
    dot_general x3, matrix products, body(): lax.dot_general(padded_grad[(2 - k) * step:(2 - k) * step + position_coun...  11.1 us
    all_to_all x1, starting transfers between devices, owner_sum(): terms = lax.all_to_all(ordered, ('y', 'x'), 0, 0, tiled=True)  7.5 us
    pallas_call x1, Pallas kernels, owner_sum(): pl.pallas_call(gradient_kernel, out_shape=jax.ShapeDtypeStruct((Y * X, Z...  6.77 us
    all_to_all x1, starting transfers between devices, owner_sum(): terms = lax.all_to_all(part.reshape(Z, rows, inner), 'z', 0, 0, tiled=True)  6.55 us
    all_to_all x1, waiting for transfers between devices, owner_sum(): terms = lax.all_to_all(part.reshape(Z, rows, inner), 'z', 0, 0, tiled=True)  4.21 us
    ppermute x2, starting transfers between devices, neighbours(): before = lax.ppermute(tail, SEQ, [(i, i + 1) for i in range(count - 1)])  3.96 us
  transfers between devices with their start and end apart: 8, of which 3 were waited for; matrix products, arithmetic and copies ran while one was open for 21% of the time, Pallas kernels for 0%

profile of v2, /device:TPU:8, one launch (start us, length us, event | category | flops | bytes accessed | tf_op | source)
XLA Modules:
  0.0 78.1 jit_solution(17438947779574433354)
XLA Ops:
  0.6 0.9 %slice_bitcast_fusion.1 = (bf16[16,1536]{1,0:T(8,128)(2,1)S(1)}, bf16[16,1536]{1,0:T(8,128)(2,1)S(1)}) fusion(bf16[1,256,1536]{2,1,0:T(8,128)(2,1)} %param.4), kind=kLoop, calls=%fused_computation.95 | loop fusion | bytes 196608 | tf_op jit(solution)/shard_map/slice | solution.py:100
  1.6 1.9 %collective-permute-start = (bf16[16,1536]{1,0:T(8,128)(2,1)S(1)}, bf16[16,1536]{1,0:T(8,128)(2,1)S(1)}, u32[]{:S(2)}, u32[]{:S(2)}) collective-permute-start(bf16[16,1536]{1,0:T(8,128)(2,1)S(1)} %get-tuple-element.3), channel_id=1, source_target_pairs={{0,4},{4,8},{8,12},{12,16},{16,20},{20,24},{24,28},{28,32},{32,36}... | collective-permute-start | bytes 147464 | tf_op jit(solution)/shard_map/ppermute | solution.py:17
  3.5 7.1 %collective-permute-start.1 = (bf16[16,1536]{1,0:T(8,128)(2,1)S(1)}, bf16[16,1536]{1,0:T(8,128)(2,1)S(1)}, u32[]{:S(2)}, u32[]{:S(2)}) collective-permute-start(bf16[16,1536]{1,0:T(8,128)(2,1)S(1)} %get-tuple-element.4), channel_id=1, source_target_pairs={{4,0},{8,4},{12,8},{16,12},{20,16},{24,20},{28,24},{32,28},{36,32}... | collective-permute-start | bytes 147464 | tf_op jit(solution)/shard_map/ppermute | solution.py:18
  10.6 1.7 %fusion.30 = bf16[256,1536]{1,0:T(8,128)(2,1)S(1)} fusion(bf16[1,256,1536]{2,1,0:T(8,128)(2,1)} %param.4), kind=kLoop, calls=%fused_computation.42 | loop fusion | flops 3932160 | bytes 1572864 | tf_op jit(solution)/shard_map/convert_element_type | solution.py:27
  12.5 3.5 %fusion.17 = f32[256,384]{1,0:T(8,128)S(1)} fusion(bf16[4608,384]{1,0:T(8,128)(2,1)} %bitcast.31, bf16[16,1536]{1,0:T(8,128)(2,1)S(1)} %fusion.65, bf16[256,1536]{1,0:T(8,128)(2,1)S(1)} %fusion.30, bf16[16,1536]{1,0:T(8,128)(2,1)S(1)} %fusion.59), kind=kOutput, calls=%fused_computation.30 | convolution fusion | flops 917766144 | bytes 4816896 | tf_op jit(solution)/shard_map/dot_general | solution.py:105
  16.0 0.7 fusion.40.grad_a
  16.7 0.1 collective-permute-start.5
  16.8 0.5 collective-permute-start.4
  17.3 1.2 %fusion.11.select = bf16[576,1152]{1,0:T(8,128)(2,1)S(1)} fusion(s32[576]{0:T(1024)S(1)} %get-tuple-element.8, s32[576]{0:T(1024)S(1)} %get-tuple-element.10, s32[576]{0:T(1024)S(1)} %get-tuple-element.9, s32[576]{0:T(1024)S(1)} %get-tuple-element.13, s32[]{:T(128)S(6)} %axis_index.15, s32[576]{0:T(1024)S(1)} %get-tuple-element.7, ...), kind=kLoop, calls=%fused_computation.23 | loop fusion | flops 14598144 | bytes 1342660 | tf_op jit(solution)/shard_map/convert_element_type | solution.py:45
  18.5 1.0 %collective-permute-done.4.act_b = bf16[288,1536]{1,0:T(8,128)(2,1)S(1)} collective-permute-done((bf16[288,1536]{1,0:T(8,128)(2,1)S(1)}, bf16[288,1536]{1,0:T(8,128)(2,1)S(1)}, u32[]{:S(2)}, u32[]{:S(2)}) %collective-permute-start.4) | collective-permute-done | bytes 884768 | tf_op jit(solution)/shard_map/ppermute | solution.py:23
  19.5 6.8 %shard_map.67 = bf16[16,144,384]{2,1,0:T(8,128)(2,1)} custom-call(bf16[288,1536]{1,0:T(8,128)(2,1)S(1)} %pad_maximum_fusion.2.act_a, bf16[288,1536]{1,0:T(8,128)(2,1)S(1)} %collective-permute-done.4.act_b, bf16[256,384]{1,0:T(8,128)(2,1)S(1)} %fusion.40.grad_a, bf16[256,384]{1,0:T(8,128)(2,1)S(1)} %collective-permute-done.5.grad_b, ...), custom_call_target="tpu_custom_call" | custom-call | flops 4000000000 | bytes 6000000 | tf_op jit(solution)/shard_map/pallas_call | solution.py:78
  26.3 7.5 %all-to-all-start = ((bf16[16,144,384]{2,1,0:T(8,128)(2,1)}), bf16[16,144,384]{2,1,0:T(8,128)(2,1)S(1)}, u32[]{:S(2)}, u32[]{:S(2)}) async-start(bf16[16,144,384]{2,1,0:T(8,128)(2,1)} %shard_map.67), calls=%async_computation | async-start | bytes 3538944 | tf_op jit(solution)/shard_map/all_to_all | solution.py:88
  33.8 2.1 %collective-permute-start.3 = (bf16[16,384]{1,0:T(8,128)(2,1)S(1)}, bf16[16,384]{1,0:T(8,128)(2,1)S(1)}, u32[]{:S(2)}, u32[]{:S(2)}) collective-permute-start(bf16[16,384]{1,0:T(8,128)(2,1)S(1)} %get-tuple-element.6), channel_id=1, source_target_pairs={{0,4},{4,8},{8,12},{12,16},{16,20},{20,24},{24,28},{28,32},{32,36}... | collective-permute-start | bytes 36872 | tf_op jit(solution)/shard_map/ppermute | solution.py:17
  35.9 3.0 %fusion.34 = f32[256,1536]{1,0:T(8,128)} fusion(bf16[256,384]{1,0:T(8,128)(2,1)S(1)} %fusion.40.grad_a, bf16[3,1536,384]{2,1,0:T(8,128)(2,1)} %param.6), kind=kOutput, calls=%fused_computation.47 | convolution fusion | flops 301989888 | bytes 2949120 | tf_op jit(solution)/shard_map/dot_general | solution.py:121
  38.9 1.5 %fusion.14 = bf16[1,256,1536]{2,1,0:T(8,128)(2,1)} fusion(bf16[384,1536]{1,0:T(8,128)(2,1)S(1)} %copy-done, bf16[1,256,1536]{2,1,0:T(8,128)(2,1)S(1)} %copy-done.1, f32[256,384]{1,0:T(8,128)S(1)} %fusion.17), kind=kOutput, calls=%fused_computation.26 | convolution fusion | flops 304054272 | bytes 3145728 | tf_op jit(solution)/shard_map/dot_general | solution.py:118
  40.4 5.7 %collective-permute-start.2 = (bf16[16,384]{1,0:T(8,128)(2,1)S(1)}, bf16[16,384]{1,0:T(8,128)(2,1)S(1)}, u32[]{:S(2)}, u32[]{:S(2)}) collective-permute-start(bf16[16,384]{1,0:T(8,128)(2,1)S(1)} %get-tuple-element.5), channel_id=1, source_target_pairs={{4,0},{8,4},{12,8},{16,12},{20,16},{24,20},{28,24},{32,28},{36,32}... | collective-permute-start | bytes 36872 | tf_op jit(solution)/shard_map/ppermute | solution.py:18
  46.1 3.0 %fusion.32 = f32[256,1536]{1,0:T(8,128)} fusion(bf16[3,1536,384]{2,1,0:T(8,128)(2,1)} %param.6, bf16[256,384]{1,0:T(8,128)(2,1)S(1)} %fusion.40.grad_a, bf16[16,384]{1,0:T(8,128)(2,1)S(1)} %collective-permute-done.3), kind=kOutput, calls=%fused_computation.45 | convolution fusion | flops 302383104 | bytes 2961408 | tf_op jit(solution)/shard_map/dot_general | solution.py:121
  49.1 11.5 %all-to-all-done = bf16[16,144,384]{2,1,0:T(8,128)(2,1)S(1)} async-done(((bf16[16,144,384]{2,1,0:T(8,128)(2,1)}), bf16[16,144,384]{2,1,0:T(8,128)(2,1)S(1)}, u32[]{:S(2)}, u32[]{:S(2)}) %all-to-all-start) | async-done | bytes 1769504 | tf_op jit(solution)/shard_map/all_to_all | solution.py:88
  60.7 0.2 reduce_sum.21
  60.9 0.7 reshape.20
  61.6 6.5 %all-to-all-start.1 = ((bf16[8,18,384]{2,1,0:T(8,128)(2,1)}), bf16[8,18,384]{2,1,0:T(8,128)(2,1)S(1)}, u32[]{:S(2)}, u32[]{:S(2)}) async-start(bf16[8,18,384]{2,1,0:T(8,128)(2,1)} %reshape.20), calls=%async_computation.1 | async-start | bytes 294912 | tf_op jit(solution)/shard_map/all_to_all | solution.py:90
  68.2 5.0 %fusion.15 = bf16[1,256,1536]{2,1,0:T(8,128)(2,1)} fusion(f32[256,1536]{1,0:T(8,128)} %fusion.32, f32[256,1536]{1,0:T(8,128)} %fusion.34, bf16[3,1536,384]{2,1,0:T(8,128)(2,1)} %param.6, bf16[1,256,1536]{2,1,0:T(8,128)(2,1)} %param.5, bf16[1,256,1536]{2,1,0:T(8,128)(2,1)} %param.4, bf16[16,384]{1,0:T(8,128)(2,1)S(1)} %collective-permute-done.2, ...), kind=kOutput, calls=%fused_computation.27 | convolution fusion | flops 311820288 | bytes 6893568 | tf_op jit(solution)/shard_map/dot_general | solution.py:121
  73.2 4.2 %all-to-all-done.1 = bf16[8,18,384]{2,1,0:T(8,128)(2,1)S(1)} async-done(((bf16[8,18,384]{2,1,0:T(8,128)(2,1)}), bf16[8,18,384]{2,1,0:T(8,128)(2,1)S(1)}, u32[]{:S(2)}, u32[]{:S(2)}) %all-to-all-start.1) | async-done | bytes 110624 | tf_op jit(solution)/shard_map/all_to_all | solution.py:90
  77.5 0.6 mul.180
  (22 shorter events, 0.3 us)
Async XLA Ops:
  0.6 15.4 %copy-start = (bf16[384,1536]{1,0:T(8,128)(2,1)S(1)}, bf16[384,1536]{1,0:T(8,128)(2,1)}, u32[]{:S(2)}) copy-start(bf16[384,1536]{1,0:T(8,128)(2,1)} %param.7) | copy-start | bytes 3538948
  1.6 10.8 %collective-permute-start = (bf16[16,1536]{1,0:T(8,128)(2,1)S(1)}, bf16[16,1536]{1,0:T(8,128)(2,1)S(1)}, u32[]{:S(2)}, u32[]{:S(2)}) collective-permute-start(bf16[16,1536]{1,0:T(8,128)(2,1)S(1)} %get-tuple-element.3), channel_id=1, source_target_pairs={{0,4},{4,8},{8,12},{12,16},{16,20},{20,24},{24,28},{28,32},{32,36}... | collective-permute-start | bytes 147464 | tf_op jit(solution)/shard_map/ppermute | solution.py:17
  3.5 8.9 %collective-permute-start.1 = (bf16[16,1536]{1,0:T(8,128)(2,1)S(1)}, bf16[16,1536]{1,0:T(8,128)(2,1)S(1)}, u32[]{:S(2)}, u32[]{:S(2)}) collective-permute-start(bf16[16,1536]{1,0:T(8,128)(2,1)S(1)} %get-tuple-element.4), channel_id=1, source_target_pairs={{4,0},{8,4},{12,8},{16,12},{20,16},{24,20},{28,24},{32,28},{36,32}... | collective-permute-start | bytes 147464 | tf_op jit(solution)/shard_map/ppermute | solution.py:18
  12.5 3.5 %copy-start.2 = (bf16[1,256,1536]{2,1,0:T(8,128)(2,1)S(1)}, bf16[1,256,1536]{2,1,0:T(8,128)(2,1)}, u32[]{:S(2)}) copy-start(bf16[1,256,1536]{2,1,0:T(8,128)(2,1)} %param.5) | copy-start | bytes 2359300
  16.7 1.8 %collective-permute-start.5 = (bf16[256,384]{1,0:T(8,128)(2,1)S(1)}, bf16[256,384]{1,0:T(8,128)(2,1)S(1)}, u32[]{:S(2)}, u32[]{:S(2)}) collective-permute-start(bf16[256,384]{1,0:T(8,128)(2,1)S(1)} %fusion.40.grad_a), channel_id=1, source_target_pairs={{0,4},{4,0},{1,5},{5,1},{2,6},{6,2},{3,7},{7,3},{8,12},{12,8},{9,1... | collective-permute-start | bytes 589832 | tf_op jit(solution)/shard_map/ppermute | solution.py:23
  16.8 2.7 %collective-permute-start.4 = (bf16[288,1536]{1,0:T(8,128)(2,1)S(1)}, bf16[288,1536]{1,0:T(8,128)(2,1)S(1)}, u32[]{:S(2)}, u32[]{:S(2)}) collective-permute-start(bf16[288,1536]{1,0:T(8,128)(2,1)S(1)} %pad_maximum_fusion.2.act_a), channel_id=1, source_target_pairs={{0,4},{4,0},{1,5},{5,1},{2,6},{6,2},{3,7},{7,3},{8,12},{12,8},{9,1... | collective-permute-start | bytes 2654216 | tf_op jit(solution)/shard_map/ppermute | solution.py:23
  26.3 34.4 %all-to-all-start = ((bf16[16,144,384]{2,1,0:T(8,128)(2,1)}), bf16[16,144,384]{2,1,0:T(8,128)(2,1)S(1)}, u32[]{:S(2)}, u32[]{:S(2)}) async-start(bf16[16,144,384]{2,1,0:T(8,128)(2,1)} %shard_map.67), calls=%async_computation | async-start | bytes 3538944 | tf_op jit(solution)/shard_map/all_to_all | solution.py:88
  33.8 5.1 %copy-start.1 = (bf16[1,256,1536]{2,1,0:T(8,128)(2,1)S(1)}, bf16[1,256,1536]{2,1,0:T(8,128)(2,1)}, u32[]{:S(2)}) copy-start(bf16[1,256,1536]{2,1,0:T(8,128)(2,1)} %param.4) | copy-start | bytes 2359300
  33.8 12.3 %collective-permute-start.3 = (bf16[16,384]{1,0:T(8,128)(2,1)S(1)}, bf16[16,384]{1,0:T(8,128)(2,1)S(1)}, u32[]{:S(2)}, u32[]{:S(2)}) collective-permute-start(bf16[16,384]{1,0:T(8,128)(2,1)S(1)} %get-tuple-element.6), channel_id=1, source_target_pairs={{0,4},{4,8},{8,12},{12,16},{16,20},{20,24},{24,28},{28,32},{32,36}... | collective-permute-start | bytes 36872 | tf_op jit(solution)/shard_map/ppermute | solution.py:17
  40.4 27.8 %collective-permute-start.2 = (bf16[16,384]{1,0:T(8,128)(2,1)S(1)}, bf16[16,384]{1,0:T(8,128)(2,1)S(1)}, u32[]{:S(2)}, u32[]{:S(2)}) collective-permute-start(bf16[16,384]{1,0:T(8,128)(2,1)S(1)} %get-tuple-element.5), channel_id=1, source_target_pairs={{4,0},{8,4},{12,8},{16,12},{20,16},{24,20},{28,24},{32,28},{36,32}... | collective-permute-start | bytes 36872 | tf_op jit(solution)/shard_map/ppermute | solution.py:18
  61.6 15.8 %all-to-all-start.1 = ((bf16[8,18,384]{2,1,0:T(8,128)(2,1)}), bf16[8,18,384]{2,1,0:T(8,128)(2,1)S(1)}, u32[]{:S(2)}, u32[]{:S(2)}) async-start(bf16[8,18,384]{2,1,0:T(8,128)(2,1)} %reshape.20), calls=%async_computation.1 | async-start | bytes 294912 | tf_op jit(solution)/shard_map/all_to_all | solution.py:90

commit v3 on v2

v3 whole, which is shorter than its diff:
```python
import math

import jax
import jax.numpy as jnp
import numpy as np
from jax import lax
from jax.experimental import pallas as pl
from jax.experimental.pallas import tpu as pltpu
from jax.sharding import Mesh, PartitionSpec as P

DILATION_STEP = 16
Y, Z, CORES, X = 4, 8, 2, 4
SEQ = ("y", "z", "core")


def next_chip_edges(edge):
    pairs = [(2 * k + 1, 2 * k + 2) for k in range(Y * Z - 1)]
    return lax.ppermute(edge, SEQ, pairs + [(b, a) for a, b in pairs])


def swap_cores(values):
    return lax.ppermute(values, "core", [(0, 1), (1, 0)])


def gelu(values):
    return jax.nn.gelu(values.astype(jnp.float32)).astype(jnp.bfloat16)


def gelu_slope(values):
    return jax.vjp(jax.nn.gelu, values)[1](jnp.ones_like(values))[0]


def shifted(padded, count):
    return jnp.concatenate(
        [padded[k * DILATION_STEP : k * DILATION_STEP + count] for k in range(3)], 1
    )


def owned_rows(rows):
    piece = 2 * rows + 4
    held = np.zeros((CORES, Z // 2, X * piece, 384), np.float32)
    for core in range(CORES):
        for z in range(Z):
            q = z // 2
            for x in range(X):
                for i in range(rows):
                    target = x * piece + 4 * (q % 2) + (z % 2) * rows + i
                    held[core, q, target, ((z * CORES + core) * X + x) * rows + i - 256 * q] = 1
    return held.astype(jnp.bfloat16)


def gradient_kernel(
    core, act_a, act_b, grad_a, grad_b, select_all, ordered, whole, select, sem
):
    fetch = pltpu.make_async_copy(select_all.at[core[0]], select, sem)
    fetch.start()
    count, inner = grad_a.shape
    channels = act_a.shape[1]
    left_a, left_b = grad_a[...].T, grad_b[...].T
    width = 512
    for j in range(3 * channels // width):
        tap, ch = divmod(j * width, channels)
        rows = slice(tap * DILATION_STEP, tap * DILATION_STEP + count)
        part = jnp.dot(
            left_a, act_a[rows, ch : ch + width], preferred_element_type=jnp.float32
        ) + jnp.dot(left_b, act_b[rows, ch : ch + width], preferred_element_type=jnp.float32)
        whole[:, j * width : (j + 1) * width] = part.astype(jnp.bfloat16)
    fetch.wait()
    pairs, piece, window = select.shape[0], select.shape[1] // X, select.shape[2]
    block = 3 * channels // Y
    for y in range(Y):
        blocks = []
        for q in range(pairs):
            start = y * block + q * 256
            blocks.append(
                lax.dot_general(
                    select[q],
                    whole[:, start : start + window],
                    (((1,), (1,)), ((), ())),
                    preferred_element_type=jnp.float32,
                )
            )
        for x in range(X):
            a, b, c, d = (held[x * piece : (x + 1) * piece] for held in blocks)
            ordered[y * X + x] = jnp.concatenate(
                [a[:32], a[32:] + b[:8], b[8:], c[:32], c[32:] + d[:8], d[8:]], 0
            ).astype(jnp.bfloat16)


def y_x_terms(act_a, act_b, grad_a, grad_b):
    inner = grad_a.shape[1]
    rows = 3 * act_a.shape[1] // (Y * Z * CORES * X)
    select = jnp.asarray(owned_rows(rows))
    vmem = pl.BlockSpec(memory_space=pltpu.VMEM)
    ordered = pl.pallas_call(
        gradient_kernel,
        out_shape=jax.ShapeDtypeStruct((Y * X, Z * rows, inner), jnp.bfloat16),
        in_specs=[pl.BlockSpec(memory_space=pltpu.SMEM)]
        + [vmem] * 4
        + [pl.BlockSpec(memory_space=pl.ANY)],
        out_specs=vmem,
        scratch_shapes=[
            pltpu.VMEM((inner, 3 * act_a.shape[1]), jnp.bfloat16),
            pltpu.VMEM(select.shape[1:], jnp.bfloat16),
            pltpu.SemaphoreType.DMA,
        ],
        compiler_params=pltpu.CompilerParams(vmem_limit_bytes=24 << 20),
        cost_estimate=pl.CostEstimate(
            flops=3 * 10**9, bytes_accessed=6 * 10**6, transcendentals=0
        ),
    )(lax.axis_index("core").astype(jnp.int32)[None], act_a, act_b, grad_a, grad_b, select)
    return lax.all_to_all(ordered, ("y", "x"), 0, 0, tiled=True)


def z_sum(terms):
    rows, inner = terms.shape[1] // Z, terms.shape[2]
    part = jnp.sum(terms.astype(jnp.float32), 0).astype(jnp.bfloat16)
    terms = lax.all_to_all(part.reshape(Z, rows, inner), "z", 0, 0, tiled=True)
    return jnp.sum(terms.astype(jnp.float32), 0).reshape(-1)


def body(inputs, cotangent, convolution_kernel, mix_weight):
    seqs, position_count, channels = inputs.shape
    x = inputs[0]
    ct = cotangent[0]
    inner = mix_weight.shape[0]
    step = DILATION_STEP
    core = lax.axis_index("core")
    last = position_count - step

    def padded(values, outer, inner):
        first = core == 0
        return jnp.concatenate(
            [jnp.where(first, outer, inner), values, jnp.where(first, inner, outer)], 0
        )

    outer = next_chip_edges(lax.dynamic_slice_in_dim(x, core * last, step, 0))
    inside = swap_cores(lax.dynamic_slice_in_dim(x, (1 - core) * last, step, 0))
    activated = padded(gelu(x), gelu(outer), gelu(inside))
    activated = lax.optimization_barrier(activated)
    activated_pair = swap_cores(activated)
    taps = shifted(activated, position_count)
    kernel_rows = convolution_kernel.reshape(3 * channels, inner)
    preact = jnp.dot(taps, kernel_rows, preferred_element_type=jnp.float32)
    preact, activated_pair = lax.optimization_barrier((preact, activated_pair))
    grad_hidden = lax.dot_general(
        ct, mix_weight, (((1,), (1,)), ((), ())), preferred_element_type=jnp.float32
    )
    pre_grad = (grad_hidden * gelu_slope(preact)).astype(jnp.bfloat16)
    pre_grad_pair = swap_cores(pre_grad)
    terms = y_x_terms(activated, activated_pair, pre_grad, pre_grad_pair)

    outer = next_chip_edges(lax.dynamic_slice_in_dim(pre_grad, core * last, step, 0))
    inside = lax.dynamic_slice_in_dim(pre_grad_pair, core * last, step, 0)
    padded_grad = padded(pre_grad, outer, inside)
    hidden = gelu(preact)
    mixed = jnp.dot(hidden, mix_weight, preferred_element_type=jnp.float32)
    outputs = (x.astype(jnp.float32) + mixed).astype(jnp.bfloat16)
    act_grad = sum(
        lax.dot_general(
            padded_grad[(2 - k) * step : (2 - k) * step + position_count],
            convolution_kernel[k],
            (((1,), (1,)), ((), ())),
            preferred_element_type=jnp.float32,
        )
        for k in range(3)
    )
    grad_inputs = (
        ct.astype(jnp.float32) + act_grad * gelu_slope(x.astype(jnp.float32))
    ).astype(jnp.bfloat16)
    terms, grad_inputs = lax.optimization_barrier((terms, grad_inputs))
    factor = 1.0 / math.sqrt(seqs * position_count * Y * Z * CORES * X)
    grad_conv = z_sum(terms) * factor
    return outputs[None], grad_inputs[None], grad_conv


def solution(mesh):
    devices = mesh.devices.reshape(Y, Z, CORES, X)
    fine = Mesh(devices, ("y", "z", "core", "x"))
    rows = P("x", SEQ, None)
    return jax.shard_map(
        body,
        mesh=fine,
        in_specs=(rows, rows, P(), P()),
        out_specs=(rows, rows, P(("y", "z", "core", "x"))),
        check_vma=False,
    )
```

time: 78.5 us -> 73.2 us (0.932)
  waiting for transfers between devices: 16.8 us -> 22.6 us
  starting transfers between devices: 31.4 us -> 25.9 us
  matrix products: 16.7 us -> 12.1 us
  Pallas kernels: 6.77 us -> 5.32 us
  local copies, waits for them, and re-layouts: 2.26 us -> 3.7 us
  other arithmetic: 3.3 us -> 2.11 us
    all_to_all x2, waiting for transfers between devices: 15.7 us -> 21.1 us  [the longest x1 14.5 us: y_x_terms(): return lax.all_to_all(ordered, ('y', 'x'), 0, 0, tiled=True)]
    ppermute x4 -> x2, starting transfers between devices: 16.8 us -> 11.9 us  [next_chip_edges(): return lax.ppermute(edge, SEQ, pairs + [(b, a) for a, b in pairs])]
    dot_general x3, matrix products: 11.1 us -> 7.41 us  [body(): lax.dot_general(padded_grad[(2 - k) * step:(2 - k) * step + position_coun...]
    dot_general x1, matrix products: 3.46 us -> 1.4 us  [body(): preact = jnp.dot(taps, kernel_rows, preferred_element_type=jnp.float32)]
    pallas_call x1, Pallas kernels: 6.77 us -> 5.32 us  [y_x_terms(): pl.pallas_call(gradient_kernel, out_shape=jax.ShapeDtypeStruct((Y * X, Z...]
    all_to_all x2, starting transfers between devices: 14.1 us -> 12.8 us  [the longest x1 7.53 us: y_x_terms(): return lax.all_to_all(ordered, ('y', 'x'), 0, 0, tiled=True)]
    unnamed x6 -> x16, local copies, waits for them, and re-layouts: 0.02 us -> 1.28 us
    convert_element_type x1 -> x0, other arithmetic: 1.15 us -> none  [owned_rows(): (source == ((z * CORES + core) * X + x) * rows + i).astype(jnp.bfloat16)]
  transfers between devices with their start and end apart: 8 -> 7, of which waited for: 3 -> 4; matrix products, arithmetic and copies ran while one was open for 21% -> 18% of each run, Pallas kernels for 0% -> 0%
where the time goes in v3:
time: 73.2 us; the launch traced here: 72.7 us
  starting transfers between devices  25.9 us (35%)
  waiting for transfers between devices  22.6 us (31%)
  matrix products  12.1 us (17%)
  Pallas kernels  5.32 us (7%)
  local copies, waits for them, and re-layouts  3.7 us (5%)
  other arithmetic  2.11 us (3%)
  between operations  0.86 us (1%)
    all_to_all x1, waiting for transfers between devices, y_x_terms(): return lax.all_to_all(ordered, ('y', 'x'), 0, 0, tiled=True)  14.5 us
    ppermute x2, starting transfers between devices, next_chip_edges(): return lax.ppermute(edge, SEQ, pairs + [(b, a) for a, b in pairs])  11.9 us
    all_to_all x1, starting transfers between devices, y_x_terms(): return lax.all_to_all(ordered, ('y', 'x'), 0, 0, tiled=True)  7.53 us
    dot_general x3, matrix products, body(): lax.dot_general(padded_grad[(2 - k) * step:(2 - k) * step + position_coun...  7.41 us
    all_to_all x1, waiting for transfers between devices, z_sum(): terms = lax.all_to_all(part.reshape(Z, rows, inner), 'z', 0, 0, tiled=True)  6.65 us
    pallas_call x1, Pallas kernels, y_x_terms(): pl.pallas_call(gradient_kernel, out_shape=jax.ShapeDtypeStruct((Y * X, Z...  5.32 us
    all_to_all x1, starting transfers between devices, z_sum(): terms = lax.all_to_all(part.reshape(Z, rows, inner), 'z', 0, 0, tiled=True)  5.25 us
    dot_general x1, matrix products, body(): mixed = jnp.dot(hidden, mix_weight, preferred_element_type=jnp.float32)  2.6 us
  transfers between devices with their start and end apart: 7, of which 4 were waited for; matrix products, arithmetic and copies ran while one was open for 18% of the time, Pallas kernels for 0%

profile of v3, /device:TPU:8, one launch (start us, length us, event | category | flops | bytes accessed | tf_op | source)
XLA Modules:
  0.0 72.7 jit_solution(1885767529150948162)
XLA Ops:
  0.7 0.9 %dynamic-slice_bitcast_fusion.1 = (bf16[16,1536]{1,0:T(8,128)(2,1)S(1)}, bf16[16,1536]{1,0:T(8,128)(2,1)S(1)}) fusion(bf16[1,256,1536]{2,1,0:T(8,128)(2,1)} %param.5, s32[]{:T(128)S(6)} %select_n.33, s32[]{:T(128)S(6)} %select_n.34), kind=kLoop, calls=%fused_computation.78 | loop fusion | bytes 196616 | tf_op jit(solution)/shard_map/dynamic_slice | solution.py:137
  1.6 7.1 %collective-permute-start = (bf16[16,1536]{1,0:T(8,128)(2,1)S(1)}, bf16[16,1536]{1,0:T(8,128)(2,1)S(1)}, u32[]{:S(2)}, u32[]{:S(2)}) collective-permute-start(bf16[16,1536]{1,0:T(8,128)(2,1)S(1)} %get-tuple-element.14), channel_id=1, source_target_pairs={{4,8},{12,16},{20,24},{28,32},{36,40},{44,48},{52,56},{60,64},{68,... | collective-permute-start | bytes 147464 | tf_op jit(solution)/shard_map/ppermute | solution.py:18
  8.8 1.7 %fusion.18 = bf16[256,1536]{1,0:T(8,128)(2,1)S(1)} fusion(bf16[1,256,1536]{2,1,0:T(8,128)(2,1)} %param.5), kind=kLoop, calls=%fused_computation.25 | loop fusion | flops 3932160 | bytes 1572864 | tf_op jit(solution)/shard_map/convert_element_type | solution.py:26
  10.6 0.6 collective-permute-start.2
  11.2 0.2 fusion.61
  11.4 1.2 %copy-done.3 = bf16[3,1536,384]{2,1,0:T(8,128)(2,1)S(1)} copy-done((bf16[3,1536,384]{2,1,0:T(8,128)(2,1)S(1)}, bf16[3,1536,384]{2,1,0:T(8,128)(2,1)}, u32[]{:S(2)}) %copy-start.3) | copy-done | bytes 3538968
  12.6 1.4 %fusion.6 = f32[256,384]{1,0:T(8,128)S(1)} fusion(bf16[4608,384]{1,0:T(8,128)(2,1)S(1)} %bitcast.31, bf16[256,1536]{1,0:T(8,128)(2,1)S(1)} %get-tuple-element.12, bf16[256,1536]{1,0:T(8,128)(2,1)S(1)} %get-tuple-element.13, bf16[256,1536]{1,0:T(8,128)(2,1)S(1)} %get-tuple-element.11), kind=kOutput, calls=%fused_computation.13 | convolution fusion | flops 913047552 | bytes 6291456 | tf_op jit(solution)/shard_map/dot_general | solution.py:144
  14.1 0.7 fusion.28.grad_a
  14.8 0.6 collective-permute-start.3
  15.4 1.1 %collective-permute-done.3.grad_b = bf16[256,384]{1,0:T(8,128)(2,1)S(1)} collective-permute-done((bf16[256,384]{1,0:T(8,128)(2,1)S(1)}, bf16[256,384]{1,0:T(8,128)(2,1)S(1)}, u32[]{:S(2)}, u32[]{:S(2)}) %collective-permute-start.3) | collective-permute-done | bytes 196640 | tf_op jit(solution)/shard_map/ppermute | solution.py:22
  16.4 5.3 %shard_map.76 = bf16[16,144,384]{2,1,0:T(8,128)(2,1)} custom-call(s32[1]{0:T(128)} %bitcast.6.core, bf16[288,1536]{1,0:T(8,128)(2,1)S(1)} %pad_maximum_fusion.act_a, bf16[288,1536]{1,0:T(8,128)(2,1)S(1)} %collective-permute-done.2.act_b, bf16[256,384]{1,0:T(8,128)(2,1)S(1)} %fusion.28.grad_a, bf16[256,384]{1,0:T(8,128)(2,1)S(1)} %collective-permute-done.3.grad_b, ...), custom_call_target="tpu_custom_call" | custom-call | flops 3000000000 | bytes 6000000 | tf_op jit(solution)/shard_map/pallas_call | solution.py:95
  21.8 7.5 %all-to-all-start = ((bf16[16,144,384]{2,1,0:T(8,128)(2,1)}), bf16[16,144,384]{2,1,0:T(8,128)(2,1)S(1)}, u32[]{:S(2)}, u32[]{:S(2)}) async-start(bf16[16,144,384]{2,1,0:T(8,128)(2,1)} %shard_map.76), calls=%async_computation | async-start | bytes 3538944 | tf_op jit(solution)/shard_map/all_to_all | solution.py:112
  29.3 4.8 %collective-permute-start.4 = (bf16[16,384]{1,0:T(8,128)(2,1)S(1)}, bf16[16,384]{1,0:T(8,128)(2,1)S(1)}, u32[]{:S(2)}, u32[]{:S(2)}) collective-permute-start(bf16[16,384]{1,0:T(8,128)(2,1)S(1)} %constant_dynamic-slice_fusion), channel_id=1, source_target_pairs={{4,8},{12,16},{20,24},{28,32},{36,40},{44,48},{52,56},{60,64},{68,... | collective-permute-start | bytes 36872 | tf_op jit(solution)/shard_map/ppermute | solution.py:18
  34.2 1.9 %fusion.22 = f32[256,1536]{1,0:T(8,128)S(1)} fusion(bf16[256,384]{1,0:T(8,128)(2,1)S(1)} %fusion.28.grad_a, bf16[3,1536,384]{2,1,0:T(8,128)(2,1)} %param.7), kind=kOutput, calls=%fused_computation.30 | convolution fusion | flops 301989888 | bytes 2949120 | tf_op jit(solution)/shard_map/dot_general | solution.py:160
  36.1 0.4 collective-permute-done.4
  36.5 1.9 %fusion.20 = f32[256,1536]{1,0:T(8,128)S(1)} fusion(bf16[3,1536,384]{2,1,0:T(8,128)(2,1)} %param.7, bf16[256,384]{1,0:T(8,128)(2,1)S(1)} %fusion.28.grad_a, bf16[16,384]{1,0:T(8,128)(2,1)S(1)} %get-tuple-element.17), kind=kOutput, calls=%fused_computation.28 | convolution fusion | flops 302383104 | bytes 2961408 | tf_op jit(solution)/shard_map/dot_general | solution.py:160
  38.4 3.7 %fusion.3 = bf16[256,1536]{1,0:T(8,128)(2,1)} fusion(f32[256,1536]{1,0:T(8,128)S(1)} %fusion.20, f32[256,1536]{1,0:T(8,128)S(1)} %fusion.22, bf16[3,1536,384]{2,1,0:T(8,128)(2,1)} %param.7, bf16[1,256,1536]{2,1,0:T(8,128)(2,1)S(1)} %copy-done.7, bf16[1,256,1536]{2,1,0:T(8,128)(2,1)S(1)} %copy-done.2, bf16[16,384]{1,0:T(8,128)(2,1)S(1)} %get-tuple-element.16, ...), kind=kOutput, calls=%fused_computation.10 | convolution fusion | flops 311820288 | bytes 6893568 | tf_op jit(solution)/shard_map/dot_general | solution.py:160
  42.1 14.5 %all-to-all-done = bf16[16,144,384]{2,1,0:T(8,128)(2,1)S(1)} async-done(((bf16[16,144,384]{2,1,0:T(8,128)(2,1)}), bf16[16,144,384]{2,1,0:T(8,128)(2,1)S(1)}, u32[]{:S(2)}, u32[]{:S(2)}) %all-to-all-start) | async-done | bytes 1769504 | tf_op jit(solution)/shard_map/all_to_all | solution.py:112
  56.6 0.2 reduce_sum.21
  56.8 0.7 reshape.20
  57.5 5.2 %all-to-all-start.1 = ((bf16[8,18,384]{2,1,0:T(8,128)(2,1)}), bf16[8,18,384]{2,1,0:T(8,128)(2,1)S(1)}, u32[]{:S(2)}, u32[]{:S(2)}) async-start(bf16[8,18,384]{2,1,0:T(8,128)(2,1)} %reshape.20), calls=%async_computation.1 | async-start | bytes 294912 | tf_op jit(solution)/shard_map/all_to_all | solution.py:118
  62.8 2.6 %fusion.5 = bf16[1,256,1536]{2,1,0:T(8,128)(2,1)} fusion(bf16[384,1536]{1,0:T(8,128)(2,1)S(1)} %copy-done, bf16[1,256,1536]{2,1,0:T(8,128)(2,1)} %param.5, f32[256,384]{1,0:T(8,128)S(1)} %copy-done.5), kind=kOutput, calls=%fused_computation.12 | convolution fusion | flops 304054272 | bytes 3145728 | tf_op jit(solution)/shard_map/dot_general | solution.py:157
  65.4 6.6 %all-to-all-done.1 = bf16[8,18,384]{2,1,0:T(8,128)(2,1)S(1)} async-done(((bf16[8,18,384]{2,1,0:T(8,128)(2,1)}), bf16[8,18,384]{2,1,0:T(8,128)(2,1)S(1)}, u32[]{:S(2)}, u32[]{:S(2)}) %all-to-all-start.1) | async-done | bytes 110624 | tf_op jit(solution)/shard_map/all_to_all | solution.py:118
  72.1 0.6 mul.169
  (25 shorter events, 0.3 us)
Async XLA Ops:
  0.6 13.4 %copy-start = (bf16[384,1536]{1,0:T(8,128)(2,1)S(1)}, bf16[384,1536]{1,0:T(8,128)(2,1)}, u32[]{:S(2)}) copy-start(bf16[384,1536]{1,0:T(8,128)(2,1)} %param.8) | copy-start | bytes 3538948
  1.6 8.9 %collective-permute-start = (bf16[16,1536]{1,0:T(8,128)(2,1)S(1)}, bf16[16,1536]{1,0:T(8,128)(2,1)S(1)}, u32[]{:S(2)}, u32[]{:S(2)}) collective-permute-start(bf16[16,1536]{1,0:T(8,128)(2,1)S(1)} %get-tuple-element.14), channel_id=1, source_target_pairs={{4,8},{12,16},{20,24},{28,32},{36,40},{44,48},{52,56},{60,64},{68,... | collective-permute-start | bytes 147464 | tf_op jit(solution)/shard_map/ppermute | solution.py:18
  8.7 1.8 %collective-permute-start.1 = (bf16[16,1536]{1,0:T(8,128)(2,1)S(1)}, bf16[16,1536]{1,0:T(8,128)(2,1)S(1)}, u32[]{:S(2)}, u32[]{:S(2)}) collective-permute-start(bf16[16,1536]{1,0:T(8,128)(2,1)S(1)} %get-tuple-element.15), channel_id=1, source_target_pairs={{0,4},{4,0},{1,5},{5,1},{2,6},{6,2},{3,7},{7,3},{8,12},{12,8},{9,1... | collective-permute-start | bytes 147464 | tf_op jit(solution)/shard_map/ppermute | solution.py:22
  10.6 2.0 %copy-start.3 = (bf16[3,1536,384]{2,1,0:T(8,128)(2,1)S(1)}, bf16[3,1536,384]{2,1,0:T(8,128)(2,1)}, u32[]{:S(2)}) copy-start(bf16[3,1536,384]{2,1,0:T(8,128)(2,1)} %param.7) | copy-start | bytes 10616836
  10.6 3.4 %collective-permute-start.2 = (bf16[288,1536]{1,0:T(8,128)(2,1)S(1)}, bf16[288,1536]{1,0:T(8,128)(2,1)S(1)}, u32[]{:S(2)}, u32[]{:S(2)}) collective-permute-start(bf16[288,1536]{1,0:T(8,128)(2,1)S(1)} %pad_maximum_fusion.act_a), channel_id=1, source_target_pairs={{0,4},{4,0},{1,5},{5,1},{2,6},{6,2},{3,7},{7,3},{8,12},{12,8},{9,1... | collective-permute-start | bytes 2654216 | tf_op jit(solution)/shard_map/ppermute | solution.py:22
  12.6 1.5 %copy-start.6 = (bf16[1,256,1536]{2,1,0:T(8,128)(2,1)S(1)}, bf16[1,256,1536]{2,1,0:T(8,128)(2,1)}, u32[]{:S(2)}) copy-start(bf16[1,256,1536]{2,1,0:T(8,128)(2,1)} %param.6) | copy-start | bytes 2359300
  14.0 0.7 %copy-start.4 = (f32[256,384]{1,0:T(8,128)}, f32[256,384]{1,0:T(8,128)S(1)}, u32[]{:S(2)}) copy-start(f32[256,384]{1,0:T(8,128)S(1)} %fusion.6) | copy-start | bytes 1179652
  14.1 2.4 %copy-start.1 = (bf16[2,4,160,384]{3,2,1,0:T(8,128)(2,1)S(1)}, bf16[2,4,160,384]{3,2,1,0:T(8,128)(2,1)}, u32[]{:S(2)}) copy-start(bf16[2,4,160,384]{3,2,1,0:T(8,128)(2,1)} %constant.46.clone.select_all) | copy-start | bytes 2949124
  14.8 1.6 %collective-permute-start.3 = (bf16[256,384]{1,0:T(8,128)(2,1)S(1)}, bf16[256,384]{1,0:T(8,128)(2,1)S(1)}, u32[]{:S(2)}, u32[]{:S(2)}) collective-permute-start(bf16[256,384]{1,0:T(8,128)(2,1)S(1)} %fusion.28.grad_a), channel_id=1, source_target_pairs={{0,4},{4,0},{1,5},{5,1},{2,6},{6,2},{3,7},{7,3},{8,12},{12,8},{9,1... | collective-permute-start | bytes 589832 | tf_op jit(solution)/shard_map/ppermute | solution.py:22
  21.8 34.8 %all-to-all-start = ((bf16[16,144,384]{2,1,0:T(8,128)(2,1)}), bf16[16,144,384]{2,1,0:T(8,128)(2,1)S(1)}, u32[]{:S(2)}, u32[]{:S(2)}) async-start(bf16[16,144,384]{2,1,0:T(8,128)(2,1)} %shard_map.76), calls=%async_computation | async-start | bytes 3538944 | tf_op jit(solution)/shard_map/all_to_all | solution.py:112
  29.3 7.2 %collective-permute-start.4 = (bf16[16,384]{1,0:T(8,128)(2,1)S(1)}, bf16[16,384]{1,0:T(8,128)(2,1)S(1)}, u32[]{:S(2)}, u32[]{:S(2)}) collective-permute-start(bf16[16,384]{1,0:T(8,128)(2,1)S(1)} %constant_dynamic-slice_fusion), channel_id=1, source_target_pairs={{4,8},{12,16},{20,24},{28,32},{36,40},{44,48},{52,56},{60,64},{68,... | collective-permute-start | bytes 36872 | tf_op jit(solution)/shard_map/ppermute | solution.py:18
  36.0 2.4 %copy-start.2 = (bf16[1,256,1536]{2,1,0:T(8,128)(2,1)S(1)}, bf16[1,256,1536]{2,1,0:T(8,128)(2,1)}, u32[]{:S(2)}) copy-start(bf16[1,256,1536]{2,1,0:T(8,128)(2,1)} %param.5) | copy-start | bytes 2359300
  36.0 2.4 %copy-start.7 = (bf16[1,256,1536]{2,1,0:T(8,128)(2,1)S(1)}, bf16[1,256,1536]{2,1,0:T(8,128)(2,1)}, u32[]{:S(2)}) copy-start(bf16[1,256,1536]{2,1,0:T(8,128)(2,1)} %param.6) | copy-start | bytes 2359300
  42.1 20.7 %copy-start.5 = (f32[256,384]{1,0:T(8,128)S(1)}, f32[256,384]{1,0:T(8,128)}, u32[]{:S(2)}) copy-start(f32[256,384]{1,0:T(8,128)} %copy-done.4) | copy-start | bytes 1179652
  57.5 14.5 %all-to-all-start.1 = ((bf16[8,18,384]{2,1,0:T(8,128)(2,1)}), bf16[8,18,384]{2,1,0:T(8,128)(2,1)S(1)}, u32[]{:S(2)}, u32[]{:S(2)}) async-start(bf16[8,18,384]{2,1,0:T(8,128)(2,1)} %reshape.20), calls=%async_computation.1 | async-start | bytes 294912 | tf_op jit(solution)/shard_map/all_to_all | solution.py:118

commit v4 on v3

--- a/solution.py
+++ b/solution.py
@@ -30,27 +30,95 @@
     return jax.vjp(jax.nn.gelu, values)[1](jnp.ones_like(values))[0]
 
 
-def shifted(padded, count):
-    return jnp.concatenate(
-        [padded[k * DILATION_STEP : k * DILATION_STEP + count] for k in range(3)], 1
-    )
-
-
 def owned_rows(rows):
-    piece = 2 * rows + 4
-    held = np.zeros((CORES, Z // 2, X * piece, 384), np.float32)
+    piece = rows + 6
+    held = np.zeros((CORES, Z, X * piece, 256), np.float32)
     for core in range(CORES):
         for z in range(Z):
-            q = z // 2
             for x in range(X):
                 for i in range(rows):
-                    target = x * piece + 4 * (q % 2) + (z % 2) * rows + i
-                    held[core, q, target, ((z * CORES + core) * X + x) * rows + i - 256 * q] = 1
+                    target = x * piece + rows * z % 8 + i
+                    held[core, z, target, ((z * CORES + core) * X + x) * rows + i - 128 * z] = 1
     return held.astype(jnp.bfloat16)
 
 
+def slope(values):
+    root, cube = 0.7978845608, 0.044715
+    square = values * values
+    wave = jnp.tanh(root * values * (1.0 + cube * square))
+    return 0.5 * (1.0 + wave) + 0.5 * values * (1.0 - wave * wave) * (
+        root * (1.0 + 3.0 * cube * square)
+    )
+
+
+def gelu_kernel(x_far, ct_far, kernel_far, mix_far, act, ct, kernel, mix, x, sems):
+    copies = [
+        pltpu.make_async_copy(source, target, sems.at[i])
+        for i, (source, target) in enumerate(
+            ((x_far, x), (kernel_far, kernel), (mix_far, mix), (ct_far, ct))
+        )
+    ]
+    for copy in copies:
+        copy.start()
+    copies[0].wait()
+    act[...] = gelu(x[...])
+    for copy in copies[1:]:
+        copy.wait()
+
+
+def gelu_and_fetch(x, ct, kernel, mix):
+    vmem = pl.BlockSpec(memory_space=pltpu.VMEM)
+    return pl.pallas_call(
+        gelu_kernel,
+        out_shape=tuple(pltpu.VMEM(a.shape, jnp.bfloat16) for a in (x, ct, kernel, mix)),
+        in_specs=[pl.BlockSpec(memory_space=pl.ANY)] * 4,
+        out_specs=(vmem,) * 4,
+        scratch_shapes=[pltpu.VMEM(x.shape, jnp.bfloat16), pltpu.SemaphoreType.DMA((4,))],
+        compiler_params=pltpu.CompilerParams(vmem_limit_bytes=24 << 20),
+        cost_estimate=pl.CostEstimate(
+            flops=4 * 10**6, bytes_accessed=7 * 10**6, transcendentals=4 * 10**5
+        ),
+    )(*(pltpu.with_memory_space_constraint(a, pltpu.HBM) for a in (x, ct, kernel, mix)))
+
+
+def pre_grad_kernel(act, ct, kernel, mix, preact, pre_grad):
+    count = ct.shape[0]
+    total = sum(
+        jnp.dot(
+            act[tap * DILATION_STEP : tap * DILATION_STEP + count],
+            kernel[tap],
+            preferred_element_type=jnp.float32,
+        )
+        for tap in range(3)
+    )
+    preact[...] = total
+    grad_hidden = lax.dot_general(
+        ct[...], mix[...], (((1,), (1,)), ((), ())), preferred_element_type=jnp.float32
+    )
+    pre_grad[...] = (grad_hidden * slope(preact[...])).astype(jnp.bfloat16)
+
+
+def preact_and_grad(act, ct, kernel, mix):
+    count, inner = ct.shape[0], mix.shape[0]
+    vmem = pl.BlockSpec(memory_space=pltpu.VMEM)
+    return pl.pallas_call(
+        pre_grad_kernel,
+        out_shape=(
+            jax.ShapeDtypeStruct((count, inner), jnp.float32),
+            jax.ShapeDtypeStruct((count, inner), jnp.bfloat16),
+        ),
+        in_specs=[vmem] * 4,
+        out_specs=(vmem, vmem),
+        compiler_params=pltpu.CompilerParams(vmem_limit_bytes=24 << 20),
+        cost_estimate=pl.CostEstimate(
+            flops=12 * 10**8, bytes_accessed=6 * 10**6, transcendentals=10**5
+        ),
+    )(act, ct, kernel, mix)
+
+
 def gradient_kernel(
-    core, act_a, act_b, grad_a, grad_b, select_all, ordered, whole, select, sem
+    core, act_a, act_b, grad_a, grad_b, select_all, ordered_far,
+    whole, select, ordered, sem, out_sems,
 ):
     fetch = pltpu.make_async_copy(select_all.at[core[0]], select, sem)
     fetch.start()
@@ -66,25 +134,35 @@
         ) + jnp.dot(left_b, act_b[rows, ch : ch + width], preferred_element_type=jnp.float32)
         whole[:, j * width : (j + 1) * width] = part.astype(jnp.bfloat16)
     fetch.wait()
-    pairs, piece, window = select.shape[0], select.shape[1] // X, select.shape[2]
+    piece, window = select.shape[1] // X, select.shape[2]
     block = 3 * channels // Y
+    stores = []
     for y in range(Y):
         blocks = []
-        for q in range(pairs):
-            start = y * block + q * 256
+        for z in range(Z):
+            start = y * block + z * 128
             blocks.append(
                 lax.dot_general(
-                    select[q],
+                    select[z],
                     whole[:, start : start + window],
                     (((1,), (1,)), ((), ())),
                     preferred_element_type=jnp.float32,
                 )
             )
         for x in range(X):
-            a, b, c, d = (held[x * piece : (x + 1) * piece] for held in blocks)
-            ordered[y * X + x] = jnp.concatenate(
-                [a[:32], a[32:] + b[:8], b[8:], c[:32], c[32:] + d[:8], d[8:]], 0
-            ).astype(jnp.bfloat16)
+            parts = []
+            for four in range(0, Z, 4):
+                a, b, c, d = (
+                    held[x * piece : (x + 1) * piece] for held in blocks[four : four + 4]
+                )
+                parts += [a[:16], a[16:] + b[:8], b[8:16], b[16:] + c[:8]]
+                parts += [c[8:16], c[16:] + d[:8], d[8:]]
+            ordered[y * X + x] = jnp.concatenate(parts, 0).astype(jnp.bfloat16)
+        span = slice(y * X, (y + 1) * X)
+        stores.append(pltpu.make_async_copy(ordered.at[span], ordered_far.at[span], out_sems.at[y]))
+        stores[-1].start()
+    for store in stores:
+        store.wait()
 
 
 def y_x_terms(act_a, act_b, grad_a, grad_b):
@@ -94,21 +172,23 @@
     vmem = pl.BlockSpec(memory_space=pltpu.VMEM)
     ordered = pl.pallas_call(
         gradient_kernel,
-        out_shape=jax.ShapeDtypeStruct((Y * X, Z * rows, inner), jnp.bfloat16),
+        out_shape=pltpu.HBM((Y * X, Z * rows, inner), jnp.bfloat16),
         in_specs=[pl.BlockSpec(memory_space=pltpu.SMEM)]
         + [vmem] * 4
         + [pl.BlockSpec(memory_space=pl.ANY)],
-        out_specs=vmem,
+        out_specs=pl.BlockSpec(memory_space=pl.ANY),
         scratch_shapes=[
             pltpu.VMEM((inner, 3 * act_a.shape[1]), jnp.bfloat16),
             pltpu.VMEM(select.shape[1:], jnp.bfloat16),
+            pltpu.VMEM((Y * X, Z * rows, inner), jnp.bfloat16),
             pltpu.SemaphoreType.DMA,
+            pltpu.SemaphoreType.DMA((Y,)),
         ],
         compiler_params=pltpu.CompilerParams(vmem_limit_bytes=24 << 20),
         cost_estimate=pl.CostEstimate(
             flops=3 * 10**9, bytes_accessed=6 * 10**6, transcendentals=0
         ),
-    )(lax.axis_index("core").astype(jnp.int32)[None], act_a, act_b, grad_a, grad_b, select)
+    )(lax.axis_index("core").astype(jnp.int32)[None], act_a, act_b, grad_a, grad_b, pltpu.with_memory_space_constraint(select, pltpu.HBM))
     return lax.all_to_all(ordered, ("y", "x"), 0, 0, tiled=True)
 
 
@@ -123,7 +203,6 @@
     seqs, position_count, channels = inputs.shape
     x = inputs[0]
     ct = cotangent[0]
-    inner = mix_weight.shape[0]
     step = DILATION_STEP
     core = lax.axis_index("core")
     last = position_count - step
@@ -136,17 +215,12 @@
 
     outer = next_chip_edges(lax.dynamic_slice_in_dim(x, core * last, step, 0))
     inside = swap_cores(lax.dynamic_slice_in_dim(x, (1 - core) * last, step, 0))
-    activated = padded(gelu(x), gelu(outer), gelu(inside))
+    act, ct_near, kernel_near, mix_near = gelu_and_fetch(x, ct, convolution_kernel, mix_weight)
+    activated = padded(act, gelu(outer), gelu(inside))
     activated = lax.optimization_barrier(activated)
     activated_pair = swap_cores(activated)
-    taps = shifted(activated, position_count)
-    kernel_rows = convolution_kernel.reshape(3 * channels, inner)
-    preact = jnp.dot(taps, kernel_rows, preferred_element_type=jnp.float32)
-    preact, activated_pair = lax.optimization_barrier((preact, activated_pair))
-    grad_hidden = lax.dot_general(
-        ct, mix_weight, (((1,), (1,)), ((), ())), preferred_element_type=jnp.float32
-    )
-    pre_grad = (grad_hidden * gelu_slope(preact)).astype(jnp.bfloat16)
+    preact, pre_grad = preact_and_grad(activated, ct_near, kernel_near, mix_near)
+    pre_grad, activated_pair = lax.optimization_barrier((pre_grad, activated_pair))
     pre_grad_pair = swap_cores(pre_grad)
     terms = y_x_terms(activated, activated_pair, pre_grad, pre_grad_pair)
 

time: 73.2 us -> 70.9 us (0.969)
  Pallas kernels: 5.32 us -> 9.54 us
  starting transfers between devices: 25.9 us -> 23.4 us
  matrix products: 12.1 us -> 10 us
  other arithmetic: 2.11 us -> 0.44 us
  local copies, waits for them, and re-layouts: 3.7 us -> 2.16 us
  waiting for transfers between devices: 22.6 us -> 24 us
    pallas_call x1 -> x3, Pallas kernels: 5.32 us -> 9.54 us  [the longest x1 4.93 us: y_x_terms(): pl.pallas_call(gradient_kernel, out_shape=pltpu.HBM((Y * X, Z * rows, inn...]
    dot_general x2 -> x0, matrix products: 2.08 us -> none  [the longest x1 1.4 us: body(): preact = jnp.dot(taps, kernel_rows, preferred_element_type=jnp.float32)]
    convert_element_type x1 -> x0, other arithmetic: 1.67 us -> none  [gelu(): return jax.nn.gelu(values.astype(jnp.float32)).astype(jnp.bfloat16)]
    unnamed x16 -> x6, local copies, waits for them, and re-layouts: 1.28 us -> 0.02 us
    ppermute x2, waiting for transfers between devices: 0.45 us -> 1.61 us  [next_chip_edges(): return lax.ppermute(edge, SEQ, pairs + [(b, a) for a, b in pairs])]
    ppermute x2, starting transfers between devices: 11.9 us -> 10.8 us  [next_chip_edges(): return lax.ppermute(edge, SEQ, pairs + [(b, a) for a, b in pairs])]
    all_to_all x1, starting transfers between devices: 5.25 us -> 4.09 us  [z_sum(): terms = lax.all_to_all(part.reshape(Z, rows, inner), 'z', 0, 0, tiled=True)]
  transfers between devices with their start and end apart: 7 -> 7, of which waited for: 4 -> 5; matrix products, arithmetic and copies ran while one was open for 18% -> 14% of each run, Pallas kernels for 0% -> 7%
where the time goes in v4:
time: 70.9 us; the launch traced here: 70.4 us
  waiting for transfers between devices  24 us (34%)
  starting transfers between devices  23.4 us (33%)
  matrix products  10 us (14%)
  Pallas kernels  9.54 us (13%)
  local copies, waits for them, and re-layouts  2.16 us (3%)
  between operations  0.8 us (1%)
    all_to_all x1, waiting for transfers between devices, y_x_terms(): return lax.all_to_all(ordered, ('y', 'x'), 0, 0, tiled=True)  14.4 us
    ppermute x2, starting transfers between devices, next_chip_edges(): return lax.ppermute(edge, SEQ, pairs + [(b, a) for a, b in pairs])  10.8 us
    all_to_all x1, starting transfers between devices, y_x_terms(): return lax.all_to_all(ordered, ('y', 'x'), 0, 0, tiled=True)  7.54 us
    dot_general x3, matrix products, body(): lax.dot_general(padded_grad[(2 - k) * step:(2 - k) * step + position_coun...  7.39 us
    all_to_all x1, waiting for transfers between devices, z_sum(): terms = lax.all_to_all(part.reshape(Z, rows, inner), 'z', 0, 0, tiled=True)  6.65 us
    pallas_call x1, Pallas kernels, y_x_terms(): pl.pallas_call(gradient_kernel, out_shape=pltpu.HBM((Y * X, Z * rows, inn...  4.93 us
    all_to_all x1, starting transfers between devices, z_sum(): terms = lax.all_to_all(part.reshape(Z, rows, inner), 'z', 0, 0, tiled=True)  4.09 us
    pallas_call x1, Pallas kernels, gelu_and_fetch(): pl.pallas_call(gelu_kernel, out_shape=tuple((pltpu.VMEM(a.shape, jnp.bflo...  2.82 us
  transfers between devices with their start and end apart: 7, of which 5 were waited for; matrix products, arithmetic and copies ran while one was open for 14% of the time, Pallas kernels for 7%

profile of v4, /device:TPU:8, one launch (start us, length us, event | category | flops | bytes accessed | tf_op | source)
XLA Modules:
  0.0 70.4 jit_solution(17846994682062295881)
XLA Ops:
  0.6 0.8 %dynamic-slice_bitcast_fusion.1 = (bf16[16,1536]{1,0:T(8,128)(2,1)S(1)}, bf16[16,1536]{1,0:T(8,128)(2,1)S(1)}) fusion(bf16[1,256,1536]{2,1,0:T(8,128)(2,1)} %param.5, s32[]{:T(128)S(6)} %select_n.33, s32[]{:T(128)S(6)} %select_n.34), kind=kLoop, calls=%fused_computation.67 | loop fusion | bytes 196616 | tf_op jit(solution)/shard_map/dynamic_slice | solution.py:216
  1.5 7.1 %collective-permute-start = (bf16[16,1536]{1,0:T(8,128)(2,1)S(1)}, bf16[16,1536]{1,0:T(8,128)(2,1)S(1)}, u32[]{:S(2)}, u32[]{:S(2)}) collective-permute-start(bf16[16,1536]{1,0:T(8,128)(2,1)S(1)} %get-tuple-element.23), channel_id=1, source_target_pairs={{4,8},{12,16},{20,24},{28,32},{36,40},{44,48},{52,56},{60,64},{68,... | collective-permute-start | bytes 147464 | tf_op jit(solution)/shard_map/ppermute | solution.py:18
  8.6 0.1 collective-permute-start.1
  8.7 2.8 %shard_map.76 = (bf16[256,1536]{1,0:T(8,128)(2,1)S(1)}, bf16[256,1536]{1,0:T(8,128)(2,1)S(1)}, bf16[3,1536,384]{2,1,0:T(8,128)(2,1)S(1)}, bf16[384,1536]{1,0:T(8,128)(2,1)S(1)}) custom-call(bf16[256,1536]{1,0:T(8,128)(2,1)} %bitcast.24, bf16[256,1536]{1,0:T(8,128)(2,1)} %bitcast.25, bf16[3,1536,384]{2,1,0:T(8,128)(2,1)} %kernel_far.1, bf16[384,1536]{1,0:T(8,128)(2,1)} %mix_far.1), custom_call_target="tpu_custom_call" | custom-call | flops 4000000 | bytes 7000000 | tf_op jit(solution)/shard_map/pallas_call | solution.py:71
  11.5 0.1 broadcast_select_fusion.1
  11.7 0.6 collective-permute-start.2
  12.2 1.8 %shard_map.77 = (f32[256,384]{1,0:T(8,128)S(1)}, bf16[256,384]{1,0:T(8,128)(2,1)S(1)}) custom-call(bf16[288,1536]{1,0:T(8,128)(2,1)S(1)} %pad_maximum_fusion.act.act_a, bf16[256,1536]{1,0:T(8,128)(2,1)S(1)} %get-tuple-element.14.ct, bf16[3,1536,384]{2,1,0:T(8,128)(2,1)S(1)} %get-tuple-element.15.kernel, bf16[384,1536]{1,0:T(8,128)(2,1)S(1)} %get-tuple-element.16.mix), custom_call_target="tpu_custom_call" | custom-call | flops 1200000000 | bytes 6000000 | tf_op jit(solution)/shard_map/pallas_call | solution.py:104
  14.0 0.3 collective-permute-done.2.act_b
  14.3 0.4 collective-permute-start.3
  14.7 1.1 %collective-permute-done.3.grad_b = bf16[256,384]{1,0:T(8,128)(2,1)S(1)} collective-permute-done((bf16[256,384]{1,0:T(8,128)(2,1)S(1)}, bf16[256,384]{1,0:T(8,128)(2,1)S(1)}, u32[]{:S(2)}, u32[]{:S(2)}) %collective-permute-start.3) | collective-permute-done | bytes 196640 | tf_op jit(solution)/shard_map/ppermute | solution.py:22
  15.7 4.9 %shard_map.78 = bf16[16,144,384]{2,1,0:T(8,128)(2,1)} custom-call(s32[1]{0:T(128)} %bitcast.5.core, bf16[288,1536]{1,0:T(8,128)(2,1)S(1)} %pad_maximum_fusion.act.act_a, bf16[288,1536]{1,0:T(8,128)(2,1)S(1)} %collective-permute-done.2.act_b, bf16[256,384]{1,0:T(8,128)(2,1)S(1)} %get-tuple-element.20.grad_a, ...), custom_call_target="tpu_custom_call" | custom-call | flops 3000000000 | bytes 6000000 | tf_op jit(solution)/shard_map/pallas_call | solution.py:173
  20.7 7.5 %all-to-all-start = ((bf16[16,144,384]{2,1,0:T(8,128)(2,1)}), bf16[16,144,384]{2,1,0:T(8,128)(2,1)S(1)}, u32[]{:S(2)}, u32[]{:S(2)}) async-start(bf16[16,144,384]{2,1,0:T(8,128)(2,1)} %shard_map.78), calls=%async_computation | async-start | bytes 3538944 | tf_op jit(solution)/shard_map/all_to_all | solution.py:192
  28.2 3.7 %collective-permute-start.4 = (bf16[16,384]{1,0:T(8,128)(2,1)S(1)}, bf16[16,384]{1,0:T(8,128)(2,1)S(1)}, u32[]{:S(2)}, u32[]{:S(2)}) collective-permute-start(bf16[16,384]{1,0:T(8,128)(2,1)S(1)} %constant_dynamic-slice_fusion), channel_id=1, source_target_pairs={{4,8},{12,16},{20,24},{28,32},{36,40},{44,48},{52,56},{60,64},{68,... | collective-permute-start | bytes 36872 | tf_op jit(solution)/shard_map/ppermute | solution.py:18
  31.9 1.9 %fusion.15 = f32[256,1536]{1,0:T(8,128)S(1)} fusion(bf16[256,384]{1,0:T(8,128)(2,1)S(1)} %get-tuple-element.20.grad_a, bf16[3,1536,384]{2,1,0:T(8,128)(2,1)} %kernel_far.1), kind=kOutput, calls=%fused_computation.21 | convolution fusion | flops 301989888 | bytes 2949120 | tf_op jit(solution)/shard_map/dot_general | solution.py:234
  33.8 1.6 %collective-permute-done.4 = bf16[16,384]{1,0:T(8,128)(2,1)S(1)} collective-permute-done((bf16[16,384]{1,0:T(8,128)(2,1)S(1)}, bf16[16,384]{1,0:T(8,128)(2,1)S(1)}, u32[]{:S(2)}, u32[]{:S(2)}) %collective-permute-start.4) | collective-permute-done | bytes 12320 | tf_op jit(solution)/shard_map/ppermute | solution.py:18
  35.4 1.9 %fusion.13 = f32[256,1536]{1,0:T(8,128)S(1)} fusion(bf16[3,1536,384]{2,1,0:T(8,128)(2,1)} %kernel_far.1, bf16[256,384]{1,0:T(8,128)(2,1)S(1)} %get-tuple-element.20.grad_a, bf16[16,384]{1,0:T(8,128)(2,1)S(1)} %get-tuple-element.26), kind=kOutput, calls=%fused_computation.19 | convolution fusion | flops 302383104 | bytes 2961408 | tf_op jit(solution)/shard_map/dot_general | solution.py:234
  37.3 3.7 %fusion.3 = bf16[256,1536]{1,0:T(8,128)(2,1)} fusion(f32[256,1536]{1,0:T(8,128)S(1)} %fusion.13, f32[256,1536]{1,0:T(8,128)S(1)} %fusion.15, bf16[3,1536,384]{2,1,0:T(8,128)(2,1)} %kernel_far.1, bf16[16,384]{1,0:T(8,128)(2,1)S(1)} %get-tuple-element.25, bf16[256,384]{1,0:T(8,128)(2,1)S(1)} %get-tuple-element.20.grad_a, ...), kind=kOutput, calls=%fused_computation.9 | convolution fusion | flops 311820288 | bytes 6893568 | tf_op jit(solution)/shard_map/dot_general | solution.py:234
  41.0 14.4 %all-to-all-done = bf16[16,144,384]{2,1,0:T(8,128)(2,1)S(1)} async-done(((bf16[16,144,384]{2,1,0:T(8,128)(2,1)}), bf16[16,144,384]{2,1,0:T(8,128)(2,1)S(1)}, u32[]{:S(2)}, u32[]{:S(2)}) %all-to-all-start) | async-done | bytes 1769504 | tf_op jit(solution)/shard_map/all_to_all | solution.py:192
  55.5 0.2 reduce_sum.21
  55.7 0.7 reshape.14
  56.4 4.1 %all-to-all-start.1 = ((bf16[8,18,384]{2,1,0:T(8,128)(2,1)}), bf16[8,18,384]{2,1,0:T(8,128)(2,1)S(1)}, u32[]{:S(2)}, u32[]{:S(2)}) async-start(bf16[8,18,384]{2,1,0:T(8,128)(2,1)} %reshape.14), calls=%async_computation.1 | async-start | bytes 294912 | tf_op jit(solution)/shard_map/all_to_all | solution.py:198
  60.5 2.6 %fusion.5 = bf16[1,256,1536]{2,1,0:T(8,128)(2,1)} fusion(bf16[384,1536]{1,0:T(8,128)(2,1)S(1)} %copy-done, f32[256,384]{1,0:T(8,128)S(1)} %get-tuple-element.17, bf16[1,256,1536]{2,1,0:T(8,128)(2,1)} %param.5), kind=kOutput, calls=%fused_computation.11 | convolution fusion | flops 304054272 | bytes 3145728 | tf_op jit(solution)/shard_map/dot_general | solution.py:231
  63.1 6.6 %all-to-all-done.1 = bf16[8,18,384]{2,1,0:T(8,128)(2,1)S(1)} async-done(((bf16[8,18,384]{2,1,0:T(8,128)(2,1)}), bf16[8,18,384]{2,1,0:T(8,128)(2,1)S(1)}, u32[]{:S(2)}, u32[]{:S(2)}) %all-to-all-start.1) | async-done | bytes 110624 | tf_op jit(solution)/shard_map/all_to_all | solution.py:198
  69.8 0.6 mul.132
  (13 shorter events, 0.1 us)
Async XLA Ops:
  1.5 10.0 %collective-permute-start = (bf16[16,1536]{1,0:T(8,128)(2,1)S(1)}, bf16[16,1536]{1,0:T(8,128)(2,1)S(1)}, u32[]{:S(2)}, u32[]{:S(2)}) collective-permute-start(bf16[16,1536]{1,0:T(8,128)(2,1)S(1)} %get-tuple-element.23), channel_id=1, source_target_pairs={{4,8},{12,16},{20,24},{28,32},{36,40},{44,48},{52,56},{60,64},{68,... | collective-permute-start | bytes 147464 | tf_op jit(solution)/shard_map/ppermute | solution.py:18
  8.6 3.0 %collective-permute-start.1 = (bf16[16,1536]{1,0:T(8,128)(2,1)S(1)}, bf16[16,1536]{1,0:T(8,128)(2,1)S(1)}, u32[]{:S(2)}, u32[]{:S(2)}) collective-permute-start(bf16[16,1536]{1,0:T(8,128)(2,1)S(1)} %get-tuple-element.24), channel_id=1, source_target_pairs={{0,4},{4,0},{1,5},{5,1},{2,6},{6,2},{3,7},{7,3},{8,12},{12,8},{9,1... | collective-permute-start | bytes 147464 | tf_op jit(solution)/shard_map/ppermute | solution.py:22
  11.7 2.6 %collective-permute-start.2 = (bf16[288,1536]{1,0:T(8,128)(2,1)S(1)}, bf16[288,1536]{1,0:T(8,128)(2,1)S(1)}, u32[]{:S(2)}, u32[]{:S(2)}) collective-permute-start(bf16[288,1536]{1,0:T(8,128)(2,1)S(1)} %pad_maximum_fusion.act.act_a), channel_id=1, source_target_pairs={{0,4},{4,0},{1,5},{5,1},{2,6},{6,2},{3,7},{7,3},{8,12},{12,8},{9,1... | collective-permute-start | bytes 2654216 | tf_op jit(solution)/shard_map/ppermute | solution.py:22
  14.3 1.4 %collective-permute-start.3 = (bf16[256,384]{1,0:T(8,128)(2,1)S(1)}, bf16[256,384]{1,0:T(8,128)(2,1)S(1)}, u32[]{:S(2)}, u32[]{:S(2)}) collective-permute-start(bf16[256,384]{1,0:T(8,128)(2,1)S(1)} %get-tuple-element.20.grad_a), channel_id=1, source_target_pairs={{0,4},{4,0},{1,5},{5,1},{2,6},{6,2},{3,7},{7,3},{8,12},{12,8},{9,1... | collective-permute-start | bytes 589832 | tf_op jit(solution)/shard_map/ppermute | solution.py:22
  20.7 34.8 %all-to-all-start = ((bf16[16,144,384]{2,1,0:T(8,128)(2,1)}), bf16[16,144,384]{2,1,0:T(8,128)(2,1)S(1)}, u32[]{:S(2)}, u32[]{:S(2)}) async-start(bf16[16,144,384]{2,1,0:T(8,128)(2,1)} %shard_map.78), calls=%async_computation | async-start | bytes 3538944 | tf_op jit(solution)/shard_map/all_to_all | solution.py:192
  28.2 7.2 %collective-permute-start.4 = (bf16[16,384]{1,0:T(8,128)(2,1)S(1)}, bf16[16,384]{1,0:T(8,128)(2,1)S(1)}, u32[]{:S(2)}, u32[]{:S(2)}) collective-permute-start(bf16[16,384]{1,0:T(8,128)(2,1)S(1)} %constant_dynamic-slice_fusion), channel_id=1, source_target_pairs={{4,8},{12,16},{20,24},{28,32},{36,40},{44,48},{52,56},{60,64},{68,... | collective-permute-start | bytes 36872 | tf_op jit(solution)/shard_map/ppermute | solution.py:18
  33.8 3.5 %copy-start.1 = (bf16[1,256,1536]{2,1,0:T(8,128)(2,1)S(1)}, bf16[1,256,1536]{2,1,0:T(8,128)(2,1)}, u32[]{:S(2)}) copy-start(bf16[1,256,1536]{2,1,0:T(8,128)(2,1)} %param.5) | copy-start | bytes 2359300
  33.8 3.5 %copy-start.2 = (bf16[1,256,1536]{2,1,0:T(8,128)(2,1)S(1)}, bf16[1,256,1536]{2,1,0:T(8,128)(2,1)}, u32[]{:S(2)}) copy-start(bf16[1,256,1536]{2,1,0:T(8,128)(2,1)} %param.6) | copy-start | bytes 2359300
  41.0 19.5 %copy-start = (bf16[384,1536]{1,0:T(8,128)(2,1)S(1)}, bf16[384,1536]{1,0:T(8,128)(2,1)}, u32[]{:S(2)}) copy-start(bf16[384,1536]{1,0:T(8,128)(2,1)} %mix_far.1) | copy-start | bytes 3538948
  56.4 13.3 %all-to-all-start.1 = ((bf16[8,18,384]{2,1,0:T(8,128)(2,1)}), bf16[8,18,384]{2,1,0:T(8,128)(2,1)S(1)}, u32[]{:S(2)}, u32[]{:S(2)}) async-start(bf16[8,18,384]{2,1,0:T(8,128)(2,1)} %reshape.14), calls=%async_computation.1 | async-start | bytes 294912 | tf_op jit(solution)/shard_map/all_to_all | solution.py:198

commit v5 on v4

--- a/solution.py
+++ b/solution.py
@@ -132,7 +132,7 @@
         part = jnp.dot(
             left_a, act_a[rows, ch : ch + width], preferred_element_type=jnp.float32
         ) + jnp.dot(left_b, act_b[rows, ch : ch + width], preferred_element_type=jnp.float32)
-        whole[:, j * width : (j + 1) * width] = part.astype(jnp.bfloat16)
+        whole[j * width : (j + 1) * width] = part.astype(jnp.bfloat16).T
     fetch.wait()
     piece, window = select.shape[1] // X, select.shape[2]
     block = 3 * channels // Y
@@ -144,8 +144,8 @@
             blocks.append(
                 lax.dot_general(
                     select[z],
-                    whole[:, start : start + window],
-                    (((1,), (1,)), ((), ())),
+                    whole[start : start + window],
+                    (((1,), (0,)), ((), ())),
                     preferred_element_type=jnp.float32,
                 )
             )
@@ -178,7 +178,7 @@
         + [pl.BlockSpec(memory_space=pl.ANY)],
         out_specs=pl.BlockSpec(memory_space=pl.ANY),
         scratch_shapes=[
-            pltpu.VMEM((inner, 3 * act_a.shape[1]), jnp.bfloat16),
+            pltpu.VMEM((3 * act_a.shape[1], inner), jnp.bfloat16),
             pltpu.VMEM(select.shape[1:], jnp.bfloat16),
             pltpu.VMEM((Y * X, Z * rows, inner), jnp.bfloat16),
             pltpu.SemaphoreType.DMA,

time: 70.9 us -> 70 us (0.987)
  Pallas kernels: 9.54 us -> 8.67 us
    pallas_call x1, Pallas kernels: 4.93 us -> 4.06 us  [y_x_terms(): pl.pallas_call(gradient_kernel, out_shape=pltpu.HBM((Y * X, Z * rows, inn...]
where the time goes in v5:
time: 70 us; the launch traced here: 69.5 us
  waiting for transfers between devices  24.1 us (34%)
  starting transfers between devices  23.4 us (33%)
  matrix products  9.99 us (14%)
  Pallas kernels  8.67 us (12%)
  local copies, waits for them, and re-layouts  2.16 us (3%)
  between operations  0.8 us (1%)
    all_to_all x1, waiting for transfers between devices, y_x_terms(): return lax.all_to_all(ordered, ('y', 'x'), 0, 0, tiled=True)  14.5 us
    ppermute x2, starting transfers between devices, next_chip_edges(): return lax.ppermute(edge, SEQ, pairs + [(b, a) for a, b in pairs])  10.8 us
    all_to_all x1, starting transfers between devices, y_x_terms(): return lax.all_to_all(ordered, ('y', 'x'), 0, 0, tiled=True)  7.54 us
    dot_general x3, matrix products, body(): lax.dot_general(padded_grad[(2 - k) * step:(2 - k) * step + position_coun...  7.39 us
    all_to_all x1, waiting for transfers between devices, z_sum(): terms = lax.all_to_all(part.reshape(Z, rows, inner), 'z', 0, 0, tiled=True)  6.65 us
    pallas_call x1, Pallas kernels, y_x_terms(): pl.pallas_call(gradient_kernel, out_shape=pltpu.HBM((Y * X, Z * rows, inn...  4.06 us
    all_to_all x1, starting transfers between devices, z_sum(): terms = lax.all_to_all(part.reshape(Z, rows, inner), 'z', 0, 0, tiled=True)  4.02 us
    pallas_call x1, Pallas kernels, gelu_and_fetch(): pl.pallas_call(gelu_kernel, out_shape=tuple((pltpu.VMEM(a.shape, jnp.bflo...  2.82 us
  transfers between devices with their start and end apart: 7, of which 5 were waited for; matrix products, arithmetic and copies ran while one was open for 14% of the time, Pallas kernels for 7%

profile of v5, /device:TPU:8, one launch (start us, length us, event | category | flops | bytes accessed | tf_op | source)
XLA Modules:
  0.0 69.5 jit_solution(10219564852962721171)
XLA Ops:
  0.6 0.8 %dynamic-slice_bitcast_fusion.1 = (bf16[16,1536]{1,0:T(8,128)(2,1)S(1)}, bf16[16,1536]{1,0:T(8,128)(2,1)S(1)}) fusion(bf16[1,256,1536]{2,1,0:T(8,128)(2,1)} %param.5, s32[]{:T(128)S(6)} %select_n.33, s32[]{:T(128)S(6)} %select_n.34), kind=kLoop, calls=%fused_computation.67 | loop fusion | bytes 196616 | tf_op jit(solution)/shard_map/dynamic_slice | solution.py:216
  1.5 7.1 %collective-permute-start = (bf16[16,1536]{1,0:T(8,128)(2,1)S(1)}, bf16[16,1536]{1,0:T(8,128)(2,1)S(1)}, u32[]{:S(2)}, u32[]{:S(2)}) collective-permute-start(bf16[16,1536]{1,0:T(8,128)(2,1)S(1)} %get-tuple-element.23), channel_id=1, source_target_pairs={{4,8},{12,16},{20,24},{28,32},{36,40},{44,48},{52,56},{60,64},{68,... | collective-permute-start | bytes 147464 | tf_op jit(solution)/shard_map/ppermute | solution.py:18
  8.6 0.1 collective-permute-start.1
  8.7 2.8 %shard_map.76 = (bf16[256,1536]{1,0:T(8,128)(2,1)S(1)}, bf16[256,1536]{1,0:T(8,128)(2,1)S(1)}, bf16[3,1536,384]{2,1,0:T(8,128)(2,1)S(1)}, bf16[384,1536]{1,0:T(8,128)(2,1)S(1)}) custom-call(bf16[256,1536]{1,0:T(8,128)(2,1)} %bitcast.24, bf16[256,1536]{1,0:T(8,128)(2,1)} %bitcast.25, bf16[3,1536,384]{2,1,0:T(8,128)(2,1)} %kernel_far.1, bf16[384,1536]{1,0:T(8,128)(2,1)} %mix_far.1), custom_call_target="tpu_custom_call" | custom-call | flops 4000000 | bytes 7000000 | tf_op jit(solution)/shard_map/pallas_call | solution.py:71
  11.5 0.1 broadcast_select_fusion.1
  11.7 0.6 collective-permute-start.2
  12.2 1.8 %shard_map.77 = (f32[256,384]{1,0:T(8,128)S(1)}, bf16[256,384]{1,0:T(8,128)(2,1)S(1)}) custom-call(bf16[288,1536]{1,0:T(8,128)(2,1)S(1)} %pad_maximum_fusion.act.act_a, bf16[256,1536]{1,0:T(8,128)(2,1)S(1)} %get-tuple-element.14.ct, bf16[3,1536,384]{2,1,0:T(8,128)(2,1)S(1)} %get-tuple-element.15.kernel, bf16[384,1536]{1,0:T(8,128)(2,1)S(1)} %get-tuple-element.16.mix), custom_call_target="tpu_custom_call" | custom-call | flops 1200000000 | bytes 6000000 | tf_op jit(solution)/shard_map/pallas_call | solution.py:104
  14.0 0.3 collective-permute-done.2.act_b
  14.3 0.4 collective-permute-start.3
  14.7 1.1 %collective-permute-done.3.grad_b = bf16[256,384]{1,0:T(8,128)(2,1)S(1)} collective-permute-done((bf16[256,384]{1,0:T(8,128)(2,1)S(1)}, bf16[256,384]{1,0:T(8,128)(2,1)S(1)}, u32[]{:S(2)}, u32[]{:S(2)}) %collective-permute-start.3) | collective-permute-done | bytes 196640 | tf_op jit(solution)/shard_map/ppermute | solution.py:22
  15.7 4.1 %shard_map.78 = bf16[16,144,384]{2,1,0:T(8,128)(2,1)} custom-call(s32[1]{0:T(128)} %bitcast.5.core, bf16[288,1536]{1,0:T(8,128)(2,1)S(1)} %pad_maximum_fusion.act.act_a, bf16[288,1536]{1,0:T(8,128)(2,1)S(1)} %collective-permute-done.2.act_b, bf16[256,384]{1,0:T(8,128)(2,1)S(1)} %get-tuple-element.20.grad_a, ...), custom_call_target="tpu_custom_call" | custom-call | flops 3000000000 | bytes 6000000 | tf_op jit(solution)/shard_map/pallas_call | solution.py:173
  19.8 7.5 %all-to-all-start = ((bf16[16,144,384]{2,1,0:T(8,128)(2,1)}), bf16[16,144,384]{2,1,0:T(8,128)(2,1)S(1)}, u32[]{:S(2)}, u32[]{:S(2)}) async-start(bf16[16,144,384]{2,1,0:T(8,128)(2,1)} %shard_map.78), calls=%async_computation | async-start | bytes 3538944 | tf_op jit(solution)/shard_map/all_to_all | solution.py:192
  27.4 3.7 %collective-permute-start.4 = (bf16[16,384]{1,0:T(8,128)(2,1)S(1)}, bf16[16,384]{1,0:T(8,128)(2,1)S(1)}, u32[]{:S(2)}, u32[]{:S(2)}) collective-permute-start(bf16[16,384]{1,0:T(8,128)(2,1)S(1)} %constant_dynamic-slice_fusion), channel_id=1, source_target_pairs={{4,8},{12,16},{20,24},{28,32},{36,40},{44,48},{52,56},{60,64},{68,... | collective-permute-start | bytes 36872 | tf_op jit(solution)/shard_map/ppermute | solution.py:18
  31.1 1.9 %fusion.15 = f32[256,1536]{1,0:T(8,128)S(1)} fusion(bf16[256,384]{1,0:T(8,128)(2,1)S(1)} %get-tuple-element.20.grad_a, bf16[3,1536,384]{2,1,0:T(8,128)(2,1)} %kernel_far.1), kind=kOutput, calls=%fused_computation.21 | convolution fusion | flops 301989888 | bytes 2949120 | tf_op jit(solution)/shard_map/dot_general | solution.py:234
  33.0 1.6 %collective-permute-done.4 = bf16[16,384]{1,0:T(8,128)(2,1)S(1)} collective-permute-done((bf16[16,384]{1,0:T(8,128)(2,1)S(1)}, bf16[16,384]{1,0:T(8,128)(2,1)S(1)}, u32[]{:S(2)}, u32[]{:S(2)}) %collective-permute-start.4) | collective-permute-done | bytes 12320 | tf_op jit(solution)/shard_map/ppermute | solution.py:18
  34.6 1.9 %fusion.13 = f32[256,1536]{1,0:T(8,128)S(1)} fusion(bf16[3,1536,384]{2,1,0:T(8,128)(2,1)} %kernel_far.1, bf16[256,384]{1,0:T(8,128)(2,1)S(1)} %get-tuple-element.20.grad_a, bf16[16,384]{1,0:T(8,128)(2,1)S(1)} %get-tuple-element.26), kind=kOutput, calls=%fused_computation.19 | convolution fusion | flops 302383104 | bytes 2961408 | tf_op jit(solution)/shard_map/dot_general | solution.py:234
  36.5 3.7 %fusion.3 = bf16[256,1536]{1,0:T(8,128)(2,1)} fusion(f32[256,1536]{1,0:T(8,128)S(1)} %fusion.13, f32[256,1536]{1,0:T(8,128)S(1)} %fusion.15, bf16[3,1536,384]{2,1,0:T(8,128)(2,1)} %kernel_far.1, bf16[16,384]{1,0:T(8,128)(2,1)S(1)} %get-tuple-element.25, bf16[256,384]{1,0:T(8,128)(2,1)S(1)} %get-tuple-element.20.grad_a, ...), kind=kOutput, calls=%fused_computation.9 | convolution fusion | flops 311820288 | bytes 6893568 | tf_op jit(solution)/shard_map/dot_general | solution.py:234
  40.1 14.5 %all-to-all-done = bf16[16,144,384]{2,1,0:T(8,128)(2,1)S(1)} async-done(((bf16[16,144,384]{2,1,0:T(8,128)(2,1)}), bf16[16,144,384]{2,1,0:T(8,128)(2,1)S(1)}, u32[]{:S(2)}, u32[]{:S(2)}) %all-to-all-start) | async-done | bytes 1769504 | tf_op jit(solution)/shard_map/all_to_all | solution.py:192
  54.6 0.2 reduce_sum.21
  54.9 0.7 reshape.14
  55.6 4.0 %all-to-all-start.1 = ((bf16[8,18,384]{2,1,0:T(8,128)(2,1)}), bf16[8,18,384]{2,1,0:T(8,128)(2,1)S(1)}, u32[]{:S(2)}, u32[]{:S(2)}) async-start(bf16[8,18,384]{2,1,0:T(8,128)(2,1)} %reshape.14), calls=%async_computation.1 | async-start | bytes 294912 | tf_op jit(solution)/shard_map/all_to_all | solution.py:198
  59.6 2.6 %fusion.5 = bf16[1,256,1536]{2,1,0:T(8,128)(2,1)} fusion(bf16[384,1536]{1,0:T(8,128)(2,1)S(1)} %copy-done, f32[256,384]{1,0:T(8,128)S(1)} %get-tuple-element.17, bf16[1,256,1536]{2,1,0:T(8,128)(2,1)} %param.5), kind=kOutput, calls=%fused_computation.11 | convolution fusion | flops 304054272 | bytes 3145728 | tf_op jit(solution)/shard_map/dot_general | solution.py:231
  62.2 6.6 %all-to-all-done.1 = bf16[8,18,384]{2,1,0:T(8,128)(2,1)S(1)} async-done(((bf16[8,18,384]{2,1,0:T(8,128)(2,1)}), bf16[8,18,384]{2,1,0:T(8,128)(2,1)S(1)}, u32[]{:S(2)}, u32[]{:S(2)}) %all-to-all-start.1) | async-done | bytes 110624 | tf_op jit(solution)/shard_map/all_to_all | solution.py:198
  68.9 0.6 mul.132
  (13 shorter events, 0.1 us)
Async XLA Ops:
  1.5 10.0 %collective-permute-start = (bf16[16,1536]{1,0:T(8,128)(2,1)S(1)}, bf16[16,1536]{1,0:T(8,128)(2,1)S(1)}, u32[]{:S(2)}, u32[]{:S(2)}) collective-permute-start(bf16[16,1536]{1,0:T(8,128)(2,1)S(1)} %get-tuple-element.23), channel_id=1, source_target_pairs={{4,8},{12,16},{20,24},{28,32},{36,40},{44,48},{52,56},{60,64},{68,... | collective-permute-start | bytes 147464 | tf_op jit(solution)/shard_map/ppermute | solution.py:18
  8.6 3.0 %collective-permute-start.1 = (bf16[16,1536]{1,0:T(8,128)(2,1)S(1)}, bf16[16,1536]{1,0:T(8,128)(2,1)S(1)}, u32[]{:S(2)}, u32[]{:S(2)}) collective-permute-start(bf16[16,1536]{1,0:T(8,128)(2,1)S(1)} %get-tuple-element.24), channel_id=1, source_target_pairs={{0,4},{4,0},{1,5},{5,1},{2,6},{6,2},{3,7},{7,3},{8,12},{12,8},{9,1... | collective-permute-start | bytes 147464 | tf_op jit(solution)/shard_map/ppermute | solution.py:22
  11.7 2.6 %collective-permute-start.2 = (bf16[288,1536]{1,0:T(8,128)(2,1)S(1)}, bf16[288,1536]{1,0:T(8,128)(2,1)S(1)}, u32[]{:S(2)}, u32[]{:S(2)}) collective-permute-start(bf16[288,1536]{1,0:T(8,128)(2,1)S(1)} %pad_maximum_fusion.act.act_a), channel_id=1, source_target_pairs={{0,4},{4,0},{1,5},{5,1},{2,6},{6,2},{3,7},{7,3},{8,12},{12,8},{9,1... | collective-permute-start | bytes 2654216 | tf_op jit(solution)/shard_map/ppermute | solution.py:22
  14.3 1.4 %collective-permute-start.3 = (bf16[256,384]{1,0:T(8,128)(2,1)S(1)}, bf16[256,384]{1,0:T(8,128)(2,1)S(1)}, u32[]{:S(2)}, u32[]{:S(2)}) collective-permute-start(bf16[256,384]{1,0:T(8,128)(2,1)S(1)} %get-tuple-element.20.grad_a), channel_id=1, source_target_pairs={{0,4},{4,0},{1,5},{5,1},{2,6},{6,2},{3,7},{7,3},{8,12},{12,8},{9,1... | collective-permute-start | bytes 589832 | tf_op jit(solution)/shard_map/ppermute | solution.py:22
  19.8 34.8 %all-to-all-start = ((bf16[16,144,384]{2,1,0:T(8,128)(2,1)}), bf16[16,144,384]{2,1,0:T(8,128)(2,1)S(1)}, u32[]{:S(2)}, u32[]{:S(2)}) async-start(bf16[16,144,384]{2,1,0:T(8,128)(2,1)} %shard_map.78), calls=%async_computation | async-start | bytes 3538944 | tf_op jit(solution)/shard_map/all_to_all | solution.py:192
  27.4 7.2 %collective-permute-start.4 = (bf16[16,384]{1,0:T(8,128)(2,1)S(1)}, bf16[16,384]{1,0:T(8,128)(2,1)S(1)}, u32[]{:S(2)}, u32[]{:S(2)}) collective-permute-start(bf16[16,384]{1,0:T(8,128)(2,1)S(1)} %constant_dynamic-slice_fusion), channel_id=1, source_target_pairs={{4,8},{12,16},{20,24},{28,32},{36,40},{44,48},{52,56},{60,64},{68,... | collective-permute-start | bytes 36872 | tf_op jit(solution)/shard_map/ppermute | solution.py:18
  32.9 3.5 %copy-start.1 = (bf16[1,256,1536]{2,1,0:T(8,128)(2,1)S(1)}, bf16[1,256,1536]{2,1,0:T(8,128)(2,1)}, u32[]{:S(2)}) copy-start(bf16[1,256,1536]{2,1,0:T(8,128)(2,1)} %param.5) | copy-start | bytes 2359300
  32.9 3.5 %copy-start.2 = (bf16[1,256,1536]{2,1,0:T(8,128)(2,1)S(1)}, bf16[1,256,1536]{2,1,0:T(8,128)(2,1)}, u32[]{:S(2)}) copy-start(bf16[1,256,1536]{2,1,0:T(8,128)(2,1)} %param.6) | copy-start | bytes 2359300
  40.1 19.5 %copy-start = (bf16[384,1536]{1,0:T(8,128)(2,1)S(1)}, bf16[384,1536]{1,0:T(8,128)(2,1)}, u32[]{:S(2)}) copy-start(bf16[384,1536]{1,0:T(8,128)(2,1)} %mix_far.1) | copy-start | bytes 3538948
  55.6 13.3 %all-to-all-start.1 = ((bf16[8,18,384]{2,1,0:T(8,128)(2,1)}), bf16[8,18,384]{2,1,0:T(8,128)(2,1)S(1)}, u32[]{:S(2)}, u32[]{:S(2)}) async-start(bf16[8,18,384]{2,1,0:T(8,128)(2,1)} %reshape.14), calls=%async_computation.1 | async-start | bytes 294912 | tf_op jit(solution)/shard_map/all_to_all | solution.py:198

commit v6 on v5

--- a/solution.py
+++ b/solution.py
@@ -242,7 +242,7 @@
     grad_inputs = (
         ct.astype(jnp.float32) + act_grad * gelu_slope(x.astype(jnp.float32))
     ).astype(jnp.bfloat16)
-    terms, grad_inputs = lax.optimization_barrier((terms, grad_inputs))
+    terms, grad_inputs, outputs = lax.optimization_barrier((terms, grad_inputs, outputs))
     factor = 1.0 / math.sqrt(seqs * position_count * Y * Z * CORES * X)
     grad_conv = z_sum(terms) * factor
     return outputs[None], grad_inputs[None], grad_conv

time: 70 us -> 69.2 us (0.989)
  blocking collectives: 0 us -> 13.1 us
  waiting for transfers between devices: 24.1 us -> 17.1 us
  starting transfers between devices: 23.4 us -> 19.5 us
  matrix products: 9.99 us -> 7.76 us
    all_to_all x0 -> x1, blocking collectives: none -> 13.1 us  [z_sum(): terms = lax.all_to_all(part.reshape(Z, rows, inner), 'z', 0, 0, tiled=True)]
    all_to_all x1 -> x0, waiting for transfers between devices: 6.65 us -> none  [z_sum(): terms = lax.all_to_all(part.reshape(Z, rows, inner), 'z', 0, 0, tiled=True)]
    all_to_all x1 -> x0, starting transfers between devices: 4.02 us -> none  [z_sum(): terms = lax.all_to_all(part.reshape(Z, rows, inner), 'z', 0, 0, tiled=True)]
    dot_general x3, matrix products: 7.39 us -> 4.87 us  [body(): lax.dot_general(padded_grad[(2 - k) * step:(2 - k) * step + position_coun...]
  transfers between devices with their start and end apart: 7 -> 6, of which waited for: 5 -> 4; matrix products, arithmetic and copies ran while one was open for 14% -> 11% of each run, Pallas kernels for 7% -> 7%
where the time goes in v6:
time: 69.2 us; the launch traced here: 68.8 us
  starting transfers between devices  19.5 us (28%)
  waiting for transfers between devices  17.1 us (25%)
  blocking collectives  13.1 us (19%)
  Pallas kernels  8.68 us (13%)
  matrix products  7.76 us (11%)
  local copies, waits for them, and re-layouts  1.51 us (2%)
  between operations  0.81 us (1%)
    all_to_all x1, waiting for transfers between devices, y_x_terms(): return lax.all_to_all(ordered, ('y', 'x'), 0, 0, tiled=True)  14.1 us
    all_to_all x1, blocking collectives, z_sum(): terms = lax.all_to_all(part.reshape(Z, rows, inner), 'z', 0, 0, tiled=True)  13.1 us
    ppermute x2, starting transfers between devices, next_chip_edges(): return lax.ppermute(edge, SEQ, pairs + [(b, a) for a, b in pairs])  10.7 us
    all_to_all x1, starting transfers between devices, y_x_terms(): return lax.all_to_all(ordered, ('y', 'x'), 0, 0, tiled=True)  7.67 us
    dot_general x3, matrix products, body(): lax.dot_general(padded_grad[(2 - k) * step:(2 - k) * step + position_coun...  4.87 us
    pallas_call x1, Pallas kernels, y_x_terms(): pl.pallas_call(gradient_kernel, out_shape=pltpu.HBM((Y * X, Z * rows, inn...  4.07 us
    dot_general x1, matrix products, body(): mixed = jnp.dot(hidden, mix_weight, preferred_element_type=jnp.float32)  2.89 us
    pallas_call x1, Pallas kernels, gelu_and_fetch(): pl.pallas_call(gelu_kernel, out_shape=tuple((pltpu.VMEM(a.shape, jnp.bflo...  2.82 us
  transfers between devices with their start and end apart: 6, of which 4 were waited for; matrix products, arithmetic and copies ran while one was open for 11% of the time, Pallas kernels for 7%

profile of v6, /device:TPU:8, one launch (start us, length us, event | category | flops | bytes accessed | tf_op | source)
XLA Modules:
  0.0 68.8 jit_solution(7589674497421564455)
XLA Ops:
  0.6 0.8 %dynamic-slice_bitcast_fusion.1 = (bf16[16,1536]{1,0:T(8,128)(2,1)S(1)}, bf16[16,1536]{1,0:T(8,128)(2,1)S(1)}) fusion(bf16[1,256,1536]{2,1,0:T(8,128)(2,1)} %param.5, s32[]{:T(128)S(6)} %select_n.33, s32[]{:T(128)S(6)} %select_n.34), kind=kLoop, calls=%fused_computation.66 | loop fusion | bytes 196616 | tf_op jit(solution)/shard_map/dynamic_slice | solution.py:216
  1.5 7.1 %collective-permute-start = (bf16[16,1536]{1,0:T(8,128)(2,1)S(1)}, bf16[16,1536]{1,0:T(8,128)(2,1)S(1)}, u32[]{:S(2)}, u32[]{:S(2)}) collective-permute-start(bf16[16,1536]{1,0:T(8,128)(2,1)S(1)} %get-tuple-element.25), channel_id=1, source_target_pairs={{4,8},{12,16},{20,24},{28,32},{36,40},{44,48},{52,56},{60,64},{68,... | collective-permute-start | bytes 147464 | tf_op jit(solution)/shard_map/ppermute | solution.py:18
  8.6 0.1 collective-permute-start.1
  8.7 2.8 %shard_map.76 = (bf16[256,1536]{1,0:T(8,128)(2,1)S(1)}, bf16[256,1536]{1,0:T(8,128)(2,1)S(1)}, bf16[3,1536,384]{2,1,0:T(8,128)(2,1)S(1)}, bf16[384,1536]{1,0:T(8,128)(2,1)S(1)}) custom-call(bf16[256,1536]{1,0:T(8,128)(2,1)} %bitcast.23, bf16[256,1536]{1,0:T(8,128)(2,1)} %bitcast.24, bf16[3,1536,384]{2,1,0:T(8,128)(2,1)} %kernel_far.1, bf16[384,1536]{1,0:T(8,128)(2,1)} %mix_far.1), custom_call_target="tpu_custom_call" | custom-call | flops 4000000 | bytes 7000000 | tf_op jit(solution)/shard_map/pallas_call | solution.py:71
  11.5 0.1 broadcast_select_fusion.1
  11.6 0.1 pad_maximum_fusion.act.act_a
  11.7 0.6 collective-permute-start.2
  12.2 1.8 %shard_map.77 = (f32[256,384]{1,0:T(8,128)S(1)}, bf16[256,384]{1,0:T(8,128)(2,1)S(1)}) custom-call(bf16[288,1536]{1,0:T(8,128)(2,1)S(1)} %pad_maximum_fusion.act.act_a, bf16[256,1536]{1,0:T(8,128)(2,1)S(1)} %get-tuple-element.15.ct, bf16[3,1536,384]{2,1,0:T(8,128)(2,1)S(1)} %get-tuple-element.16.kernel, bf16[384,1536]{1,0:T(8,128)(2,1)S(1)} %get-tuple-element.17.mix), custom_call_target="tpu_custom_call" | custom-call | flops 1200000000 | bytes 6000000 | tf_op jit(solution)/shard_map/pallas_call | solution.py:104
  14.0 0.3 collective-permute-done.2.act_b
  14.3 0.4 collective-permute-start.3
  14.7 1.1 %collective-permute-done.3.grad_b = bf16[256,384]{1,0:T(8,128)(2,1)S(1)} collective-permute-done((bf16[256,384]{1,0:T(8,128)(2,1)S(1)}, bf16[256,384]{1,0:T(8,128)(2,1)S(1)}, u32[]{:S(2)}, u32[]{:S(2)}) %collective-permute-start.3) | collective-permute-done | bytes 196640 | tf_op jit(solution)/shard_map/ppermute | solution.py:22
  15.7 4.1 %shard_map.78 = bf16[16,144,384]{2,1,0:T(8,128)(2,1)} custom-call(s32[1]{0:T(128)} %bitcast.core, bf16[288,1536]{1,0:T(8,128)(2,1)S(1)} %pad_maximum_fusion.act.act_a, bf16[288,1536]{1,0:T(8,128)(2,1)S(1)} %collective-permute-done.2.act_b, bf16[256,384]{1,0:T(8,128)(2,1)S(1)} %get-tuple-element.20.grad_a, ...), custom_call_target="tpu_custom_call" | custom-call | flops 3000000000 | bytes 6000000 | tf_op jit(solution)/shard_map/pallas_call | solution.py:173
  19.8 7.7 %all-to-all-start = ((bf16[16,144,384]{2,1,0:T(8,128)(2,1)}), bf16[16,144,384]{2,1,0:T(8,128)(2,1)S(1)}, u32[]{:S(2)}, u32[]{:S(2)}) async-start(bf16[16,144,384]{2,1,0:T(8,128)(2,1)} %shard_map.78), calls=%async_computation | async-start | bytes 3538944 | tf_op jit(solution)/shard_map/all_to_all | solution.py:192
  27.5 2.9 %fusion.4 = bf16[256,1536]{1,0:T(8,128)(2,1)} fusion(bf16[384,1536]{1,0:T(8,128)(2,1)} %mix_far.1, f32[256,384]{1,0:T(8,128)S(1)} %get-tuple-element.21, bf16[1,256,1536]{2,1,0:T(8,128)(2,1)S(1)} %copy-done.1), kind=kOutput, calls=%fused_computation.10 | convolution fusion | flops 304054272 | bytes 3145728 | tf_op jit(solution)/shard_map/dot_general | solution.py:231
  30.4 3.7 %collective-permute-start.4 = (bf16[16,384]{1,0:T(8,128)(2,1)S(1)}, bf16[16,384]{1,0:T(8,128)(2,1)S(1)}, u32[]{:S(2)}, u32[]{:S(2)}) collective-permute-start(bf16[16,384]{1,0:T(8,128)(2,1)S(1)} %constant_dynamic-slice_fusion), channel_id=1, source_target_pairs={{4,8},{12,16},{20,24},{28,32},{36,40},{44,48},{52,56},{60,64},{68,... | collective-permute-start | bytes 36872 | tf_op jit(solution)/shard_map/ppermute | solution.py:18
  34.1 1.9 %fusion.14 = f32[256,1536]{1,0:T(8,128)S(1)} fusion(bf16[256,384]{1,0:T(8,128)(2,1)S(1)} %get-tuple-element.20.grad_a, bf16[3,1536,384]{2,1,0:T(8,128)(2,1)} %kernel_far.1), kind=kOutput, calls=%fused_computation.20 | convolution fusion | flops 301989888 | bytes 2949120 | tf_op jit(solution)/shard_map/dot_general | solution.py:234
  36.0 0.0 copy-start.2
  36.0 1.6 %collective-permute-done.4 = bf16[16,384]{1,0:T(8,128)(2,1)S(1)} collective-permute-done((bf16[16,384]{1,0:T(8,128)(2,1)S(1)}, bf16[16,384]{1,0:T(8,128)(2,1)S(1)}, u32[]{:S(2)}, u32[]{:S(2)}) %collective-permute-start.4) | collective-permute-done | bytes 12320 | tf_op jit(solution)/shard_map/ppermute | solution.py:18
  37.6 0.6 fusion.12
  38.2 2.4 %fusion.3 = bf16[256,1536]{1,0:T(8,128)(2,1)} fusion(f32[256,1536]{1,0:T(8,128)S(1)} %fusion.12, f32[256,1536]{1,0:T(8,128)S(1)} %fusion.14, bf16[3,1536,384]{2,1,0:T(8,128)(2,1)S(1)} %copy-done, bf16[16,384]{1,0:T(8,128)(2,1)S(1)} %get-tuple-element.27, bf16[256,384]{1,0:T(8,128)(2,1)S(1)} %get-tuple-element.20.grad_a, ...), kind=kOutput, calls=%fused_computation.9 | convolution fusion | flops 311820288 | bytes 6893568 | tf_op jit(solution)/shard_map/dot_general | solution.py:234
  40.6 14.1 %all-to-all-done = bf16[16,144,384]{2,1,0:T(8,128)(2,1)S(1)} async-done(((bf16[16,144,384]{2,1,0:T(8,128)(2,1)}), bf16[16,144,384]{2,1,0:T(8,128)(2,1)S(1)}, u32[]{:S(2)}, u32[]{:S(2)}) %all-to-all-start) | async-done | bytes 1769504 | tf_op jit(solution)/shard_map/all_to_all | solution.py:192
  54.8 0.2 reduce_sum.21
  55.1 13.1 %all_to_all.10 = bf16[8,18,384]{2,1,0:T(8,128)(2,1)S(1)} all-to-all(bf16[8,18,384]{2,1,0:T(8,128)(2,1)S(1)} %reshape.14), channel_id=1, replica_groups=mesh['y'=4,'z'=8,'core'=2,'x'=4] {'z'}, dimensions={0} | all-to-all | bytes 221184 | tf_op jit(solution)/shard_map/all_to_all | solution.py:198
  68.2 0.6 mul.132
  (12 shorter events, 0.1 us)
Async XLA Ops:
  1.5 10.0 %collective-permute-start = (bf16[16,1536]{1,0:T(8,128)(2,1)S(1)}, bf16[16,1536]{1,0:T(8,128)(2,1)S(1)}, u32[]{:S(2)}, u32[]{:S(2)}) collective-permute-start(bf16[16,1536]{1,0:T(8,128)(2,1)S(1)} %get-tuple-element.25), channel_id=1, source_target_pairs={{4,8},{12,16},{20,24},{28,32},{36,40},{44,48},{52,56},{60,64},{68,... | collective-permute-start | bytes 147464 | tf_op jit(solution)/shard_map/ppermute | solution.py:18
  8.6 3.0 %collective-permute-start.1 = (bf16[16,1536]{1,0:T(8,128)(2,1)S(1)}, bf16[16,1536]{1,0:T(8,128)(2,1)S(1)}, u32[]{:S(2)}, u32[]{:S(2)}) collective-permute-start(bf16[16,1536]{1,0:T(8,128)(2,1)S(1)} %get-tuple-element.26), channel_id=1, source_target_pairs={{0,4},{4,0},{1,5},{5,1},{2,6},{6,2},{3,7},{7,3},{8,12},{12,8},{9,1... | collective-permute-start | bytes 147464 | tf_op jit(solution)/shard_map/ppermute | solution.py:22
  11.7 2.6 %collective-permute-start.2 = (bf16[288,1536]{1,0:T(8,128)(2,1)S(1)}, bf16[288,1536]{1,0:T(8,128)(2,1)S(1)}, u32[]{:S(2)}, u32[]{:S(2)}) collective-permute-start(bf16[288,1536]{1,0:T(8,128)(2,1)S(1)} %pad_maximum_fusion.act.act_a), channel_id=1, source_target_pairs={{0,4},{4,0},{1,5},{5,1},{2,6},{6,2},{3,7},{7,3},{8,12},{12,8},{9,1... | collective-permute-start | bytes 2654216 | tf_op jit(solution)/shard_map/ppermute | solution.py:22
  14.3 1.4 %collective-permute-start.3 = (bf16[256,384]{1,0:T(8,128)(2,1)S(1)}, bf16[256,384]{1,0:T(8,128)(2,1)S(1)}, u32[]{:S(2)}, u32[]{:S(2)}) collective-permute-start(bf16[256,384]{1,0:T(8,128)(2,1)S(1)} %get-tuple-element.20.grad_a), channel_id=1, source_target_pairs={{0,4},{4,0},{1,5},{5,1},{2,6},{6,2},{3,7},{7,3},{8,12},{12,8},{9,1... | collective-permute-start | bytes 589832 | tf_op jit(solution)/shard_map/ppermute | solution.py:22
  19.8 7.7 %copy-start.1 = (bf16[1,256,1536]{2,1,0:T(8,128)(2,1)S(1)}, bf16[1,256,1536]{2,1,0:T(8,128)(2,1)}, u32[]{:S(2)}) copy-start(bf16[1,256,1536]{2,1,0:T(8,128)(2,1)} %param.5) | copy-start | bytes 2359300
  19.8 34.9 %all-to-all-start = ((bf16[16,144,384]{2,1,0:T(8,128)(2,1)}), bf16[16,144,384]{2,1,0:T(8,128)(2,1)S(1)}, u32[]{:S(2)}, u32[]{:S(2)}) async-start(bf16[16,144,384]{2,1,0:T(8,128)(2,1)} %shard_map.78), calls=%async_computation | async-start | bytes 3538944 | tf_op jit(solution)/shard_map/all_to_all | solution.py:192
  27.5 10.1 %copy-start = (bf16[3,1536,384]{2,1,0:T(8,128)(2,1)S(1)}, bf16[3,1536,384]{2,1,0:T(8,128)(2,1)}, u32[]{:S(2)}) copy-start(bf16[3,1536,384]{2,1,0:T(8,128)(2,1)} %kernel_far.1) | copy-start | bytes 10616836
  30.4 7.2 %collective-permute-start.4 = (bf16[16,384]{1,0:T(8,128)(2,1)S(1)}, bf16[16,384]{1,0:T(8,128)(2,1)S(1)}, u32[]{:S(2)}, u32[]{:S(2)}) collective-permute-start(bf16[16,384]{1,0:T(8,128)(2,1)S(1)} %constant_dynamic-slice_fusion), channel_id=1, source_target_pairs={{4,8},{12,16},{20,24},{28,32},{36,40},{44,48},{52,56},{60,64},{68,... | collective-permute-start | bytes 36872 | tf_op jit(solution)/shard_map/ppermute | solution.py:18
  36.0 2.3 %copy-start.2 = (bf16[1,256,1536]{2,1,0:T(8,128)(2,1)S(1)}, bf16[1,256,1536]{2,1,0:T(8,128)(2,1)}, u32[]{:S(2)}) copy-start(bf16[1,256,1536]{2,1,0:T(8,128)(2,1)} %param.6) | copy-start | bytes 2359300

commit v7 on v6

--- a/solution.py
+++ b/solution.py
@@ -157,10 +157,10 @@
                 )
                 parts += [a[:16], a[16:] + b[:8], b[8:16], b[16:] + c[:8]]
                 parts += [c[8:16], c[16:] + d[:8], d[8:]]
-            ordered[y * X + x] = jnp.concatenate(parts, 0).astype(jnp.bfloat16)
-        span = slice(y * X, (y + 1) * X)
-        stores.append(pltpu.make_async_copy(ordered.at[span], ordered_far.at[span], out_sems.at[y]))
-        stores[-1].start()
+            at = x * Y + y
+            ordered[at] = jnp.concatenate(parts, 0).astype(jnp.bfloat16)
+            stores.append(pltpu.make_async_copy(ordered.at[at], ordered_far.at[at], out_sems.at[at]))
+            stores[-1].start()
     for store in stores:
         store.wait()
 
@@ -182,14 +182,14 @@
             pltpu.VMEM(select.shape[1:], jnp.bfloat16),
             pltpu.VMEM((Y * X, Z * rows, inner), jnp.bfloat16),
             pltpu.SemaphoreType.DMA,
-            pltpu.SemaphoreType.DMA((Y,)),
+            pltpu.SemaphoreType.DMA((Y * X,)),
         ],
         compiler_params=pltpu.CompilerParams(vmem_limit_bytes=24 << 20),
         cost_estimate=pl.CostEstimate(
             flops=3 * 10**9, bytes_accessed=6 * 10**6, transcendentals=0
         ),
     )(lax.axis_index("core").astype(jnp.int32)[None], act_a, act_b, grad_a, grad_b, pltpu.with_memory_space_constraint(select, pltpu.HBM))
-    return lax.all_to_all(ordered, ("y", "x"), 0, 0, tiled=True)
+    return lax.all_to_all(ordered, ("x", "y"), 0, 0, tiled=True)
 
 
 def z_sum(terms):

time: 69.2 us -> 68.3 us (0.987)
  waiting for transfers between devices: 17.1 us -> 15.9 us
    all_to_all x1, waiting for transfers between devices: 14.1 us -> 12.9 us  [y_x_terms(): return lax.all_to_all(ordered, ('x', 'y'), 0, 0, tiled=True)]
where the time goes in v7:
time: 68.3 us; the launch traced here: 67.9 us
  starting transfers between devices  19.5 us (29%)
  waiting for transfers between devices  15.9 us (23%)
  blocking collectives  13.2 us (19%)
  Pallas kernels  8.88 us (13%)
  matrix products  7.76 us (11%)
  local copies, waits for them, and re-layouts  1.51 us (2%)
  between operations  0.81 us (1%)
    all_to_all x1, blocking collectives, z_sum(): terms = lax.all_to_all(part.reshape(Z, rows, inner), 'z', 0, 0, tiled=True)  13.2 us
    all_to_all x1, waiting for transfers between devices, y_x_terms(): return lax.all_to_all(ordered, ('x', 'y'), 0, 0, tiled=True)  12.9 us
    ppermute x2, starting transfers between devices, next_chip_edges(): return lax.ppermute(edge, SEQ, pairs + [(b, a) for a, b in pairs])  10.7 us
    all_to_all x1, starting transfers between devices, y_x_terms(): return lax.all_to_all(ordered, ('x', 'y'), 0, 0, tiled=True)  7.67 us
    dot_general x3, matrix products, body(): lax.dot_general(padded_grad[(2 - k) * step:(2 - k) * step + position_coun...  4.87 us
    pallas_call x1, Pallas kernels, y_x_terms(): pl.pallas_call(gradient_kernel, out_shape=pltpu.HBM((Y * X, Z * rows, inn...  4.27 us
    dot_general x1, matrix products, body(): mixed = jnp.dot(hidden, mix_weight, preferred_element_type=jnp.float32)  2.89 us
    pallas_call x1, Pallas kernels, gelu_and_fetch(): pl.pallas_call(gelu_kernel, out_shape=tuple((pltpu.VMEM(a.shape, jnp.bflo...  2.82 us
  transfers between devices with their start and end apart: 6, of which 4 were waited for; matrix products, arithmetic and copies ran while one was open for 11% of the time, Pallas kernels for 7%

profile of v7, /device:TPU:8, one launch (start us, length us, event | category | flops | bytes accessed | tf_op | source)
XLA Modules:
  0.0 67.9 jit_solution(2264034838007107020)
XLA Ops:
  0.6 0.8 %dynamic-slice_bitcast_fusion.1 = (bf16[16,1536]{1,0:T(8,128)(2,1)S(1)}, bf16[16,1536]{1,0:T(8,128)(2,1)S(1)}) fusion(bf16[1,256,1536]{2,1,0:T(8,128)(2,1)} %param.5, s32[]{:T(128)S(6)} %select_n.33, s32[]{:T(128)S(6)} %select_n.34), kind=kLoop, calls=%fused_computation.66 | loop fusion | bytes 196616 | tf_op jit(solution)/shard_map/dynamic_slice | solution.py:216
  1.5 7.1 %collective-permute-start = (bf16[16,1536]{1,0:T(8,128)(2,1)S(1)}, bf16[16,1536]{1,0:T(8,128)(2,1)S(1)}, u32[]{:S(2)}, u32[]{:S(2)}) collective-permute-start(bf16[16,1536]{1,0:T(8,128)(2,1)S(1)} %get-tuple-element.25), channel_id=1, source_target_pairs={{4,8},{12,16},{20,24},{28,32},{36,40},{44,48},{52,56},{60,64},{68,... | collective-permute-start | bytes 147464 | tf_op jit(solution)/shard_map/ppermute | solution.py:18
  8.6 0.1 collective-permute-start.1
  8.7 2.8 %shard_map.76 = (bf16[256,1536]{1,0:T(8,128)(2,1)S(1)}, bf16[256,1536]{1,0:T(8,128)(2,1)S(1)}, bf16[3,1536,384]{2,1,0:T(8,128)(2,1)S(1)}, bf16[384,1536]{1,0:T(8,128)(2,1)S(1)}) custom-call(bf16[256,1536]{1,0:T(8,128)(2,1)} %bitcast.23, bf16[256,1536]{1,0:T(8,128)(2,1)} %bitcast.24, bf16[3,1536,384]{2,1,0:T(8,128)(2,1)} %kernel_far.1, bf16[384,1536]{1,0:T(8,128)(2,1)} %mix_far.1), custom_call_target="tpu_custom_call" | custom-call | flops 4000000 | bytes 7000000 | tf_op jit(solution)/shard_map/pallas_call | solution.py:71
  11.5 0.1 broadcast_select_fusion.1
  11.6 0.1 pad_maximum_fusion.act.act_a
  11.7 0.6 collective-permute-start.2
  12.2 1.8 %shard_map.77 = (f32[256,384]{1,0:T(8,128)S(1)}, bf16[256,384]{1,0:T(8,128)(2,1)S(1)}) custom-call(bf16[288,1536]{1,0:T(8,128)(2,1)S(1)} %pad_maximum_fusion.act.act_a, bf16[256,1536]{1,0:T(8,128)(2,1)S(1)} %get-tuple-element.15.ct, bf16[3,1536,384]{2,1,0:T(8,128)(2,1)S(1)} %get-tuple-element.16.kernel, bf16[384,1536]{1,0:T(8,128)(2,1)S(1)} %get-tuple-element.17.mix), custom_call_target="tpu_custom_call" | custom-call | flops 1200000000 | bytes 6000000 | tf_op jit(solution)/shard_map/pallas_call | solution.py:104
  14.0 0.3 collective-permute-done.2.act_b
  14.3 0.4 collective-permute-start.3
  14.7 1.1 %collective-permute-done.3.grad_b = bf16[256,384]{1,0:T(8,128)(2,1)S(1)} collective-permute-done((bf16[256,384]{1,0:T(8,128)(2,1)S(1)}, bf16[256,384]{1,0:T(8,128)(2,1)S(1)}, u32[]{:S(2)}, u32[]{:S(2)}) %collective-permute-start.3) | collective-permute-done | bytes 196640 | tf_op jit(solution)/shard_map/ppermute | solution.py:22
  15.7 4.3 %shard_map.78 = bf16[16,144,384]{2,1,0:T(8,128)(2,1)} custom-call(s32[1]{0:T(128)} %bitcast.core, bf16[288,1536]{1,0:T(8,128)(2,1)S(1)} %pad_maximum_fusion.act.act_a, bf16[288,1536]{1,0:T(8,128)(2,1)S(1)} %collective-permute-done.2.act_b, bf16[256,384]{1,0:T(8,128)(2,1)S(1)} %get-tuple-element.20.grad_a, ...), custom_call_target="tpu_custom_call" | custom-call | flops 3000000000 | bytes 6000000 | tf_op jit(solution)/shard_map/pallas_call | solution.py:173
  20.0 0.0 copy-start.1
  20.0 7.7 %all-to-all-start = ((bf16[16,144,384]{2,1,0:T(8,128)(2,1)}), bf16[16,144,384]{2,1,0:T(8,128)(2,1)S(1)}, u32[]{:S(2)}, u32[]{:S(2)}) async-start(bf16[16,144,384]{2,1,0:T(8,128)(2,1)} %shard_map.78), calls=%async_computation | async-start | bytes 3538944 | tf_op jit(solution)/shard_map/all_to_all | solution.py:192
  27.7 2.9 %fusion.4 = bf16[256,1536]{1,0:T(8,128)(2,1)} fusion(bf16[384,1536]{1,0:T(8,128)(2,1)} %mix_far.1, f32[256,384]{1,0:T(8,128)S(1)} %get-tuple-element.21, bf16[1,256,1536]{2,1,0:T(8,128)(2,1)S(1)} %copy-done.1), kind=kOutput, calls=%fused_computation.10 | convolution fusion | flops 304054272 | bytes 3145728 | tf_op jit(solution)/shard_map/dot_general | solution.py:231
  30.6 3.7 %collective-permute-start.4 = (bf16[16,384]{1,0:T(8,128)(2,1)S(1)}, bf16[16,384]{1,0:T(8,128)(2,1)S(1)}, u32[]{:S(2)}, u32[]{:S(2)}) collective-permute-start(bf16[16,384]{1,0:T(8,128)(2,1)S(1)} %constant_dynamic-slice_fusion), channel_id=1, source_target_pairs={{4,8},{12,16},{20,24},{28,32},{36,40},{44,48},{52,56},{60,64},{68,... | collective-permute-start | bytes 36872 | tf_op jit(solution)/shard_map/ppermute | solution.py:18
  34.3 1.9 %fusion.14 = f32[256,1536]{1,0:T(8,128)S(1)} fusion(bf16[256,384]{1,0:T(8,128)(2,1)S(1)} %get-tuple-element.20.grad_a, bf16[3,1536,384]{2,1,0:T(8,128)(2,1)} %kernel_far.1), kind=kOutput, calls=%fused_computation.20 | convolution fusion | flops 301989888 | bytes 2949120 | tf_op jit(solution)/shard_map/dot_general | solution.py:234
  36.2 1.6 %collective-permute-done.4 = bf16[16,384]{1,0:T(8,128)(2,1)S(1)} collective-permute-done((bf16[16,384]{1,0:T(8,128)(2,1)S(1)}, bf16[16,384]{1,0:T(8,128)(2,1)S(1)}, u32[]{:S(2)}, u32[]{:S(2)}) %collective-permute-start.4) | collective-permute-done | bytes 12320 | tf_op jit(solution)/shard_map/ppermute | solution.py:18
  37.8 0.6 fusion.12
  38.4 2.4 %fusion.3 = bf16[256,1536]{1,0:T(8,128)(2,1)} fusion(f32[256,1536]{1,0:T(8,128)S(1)} %fusion.12, f32[256,1536]{1,0:T(8,128)S(1)} %fusion.14, bf16[3,1536,384]{2,1,0:T(8,128)(2,1)S(1)} %copy-done, bf16[16,384]{1,0:T(8,128)(2,1)S(1)} %get-tuple-element.27, bf16[256,384]{1,0:T(8,128)(2,1)S(1)} %get-tuple-element.20.grad_a, ...), kind=kOutput, calls=%fused_computation.9 | convolution fusion | flops 311820288 | bytes 6893568 | tf_op jit(solution)/shard_map/dot_general | solution.py:234
  40.8 12.9 %all-to-all-done = bf16[16,144,384]{2,1,0:T(8,128)(2,1)S(1)} async-done(((bf16[16,144,384]{2,1,0:T(8,128)(2,1)}), bf16[16,144,384]{2,1,0:T(8,128)(2,1)S(1)}, u32[]{:S(2)}, u32[]{:S(2)}) %all-to-all-start) | async-done | bytes 1769504 | tf_op jit(solution)/shard_map/all_to_all | solution.py:192
  53.7 0.2 reduce_sum.21
  54.0 13.2 %all_to_all.10 = bf16[8,18,384]{2,1,0:T(8,128)(2,1)S(1)} all-to-all(bf16[8,18,384]{2,1,0:T(8,128)(2,1)S(1)} %reshape.14), channel_id=1, replica_groups=mesh['y'=4,'z'=8,'core'=2,'x'=4] {'z'}, dimensions={0} | all-to-all | bytes 221184 | tf_op jit(solution)/shard_map/all_to_all | solution.py:198
  67.3 0.6 mul.132
  (12 shorter events, 0.1 us)
Async XLA Ops:
  1.5 10.0 %collective-permute-start = (bf16[16,1536]{1,0:T(8,128)(2,1)S(1)}, bf16[16,1536]{1,0:T(8,128)(2,1)S(1)}, u32[]{:S(2)}, u32[]{:S(2)}) collective-permute-start(bf16[16,1536]{1,0:T(8,128)(2,1)S(1)} %get-tuple-element.25), channel_id=1, source_target_pairs={{4,8},{12,16},{20,24},{28,32},{36,40},{44,48},{52,56},{60,64},{68,... | collective-permute-start | bytes 147464 | tf_op jit(solution)/shard_map/ppermute | solution.py:18
  8.6 3.0 %collective-permute-start.1 = (bf16[16,1536]{1,0:T(8,128)(2,1)S(1)}, bf16[16,1536]{1,0:T(8,128)(2,1)S(1)}, u32[]{:S(2)}, u32[]{:S(2)}) collective-permute-start(bf16[16,1536]{1,0:T(8,128)(2,1)S(1)} %get-tuple-element.26), channel_id=1, source_target_pairs={{0,4},{4,0},{1,5},{5,1},{2,6},{6,2},{3,7},{7,3},{8,12},{12,8},{9,1... | collective-permute-start | bytes 147464 | tf_op jit(solution)/shard_map/ppermute | solution.py:22
  11.7 2.6 %collective-permute-start.2 = (bf16[288,1536]{1,0:T(8,128)(2,1)S(1)}, bf16[288,1536]{1,0:T(8,128)(2,1)S(1)}, u32[]{:S(2)}, u32[]{:S(2)}) collective-permute-start(bf16[288,1536]{1,0:T(8,128)(2,1)S(1)} %pad_maximum_fusion.act.act_a), channel_id=1, source_target_pairs={{0,4},{4,0},{1,5},{5,1},{2,6},{6,2},{3,7},{7,3},{8,12},{12,8},{9,1... | collective-permute-start | bytes 2654216 | tf_op jit(solution)/shard_map/ppermute | solution.py:22
  14.3 1.4 %collective-permute-start.3 = (bf16[256,384]{1,0:T(8,128)(2,1)S(1)}, bf16[256,384]{1,0:T(8,128)(2,1)S(1)}, u32[]{:S(2)}, u32[]{:S(2)}) collective-permute-start(bf16[256,384]{1,0:T(8,128)(2,1)S(1)} %get-tuple-element.20.grad_a), channel_id=1, source_target_pairs={{0,4},{4,0},{1,5},{5,1},{2,6},{6,2},{3,7},{7,3},{8,12},{12,8},{9,1... | collective-permute-start | bytes 589832 | tf_op jit(solution)/shard_map/ppermute | solution.py:22
  20.0 7.7 %copy-start.1 = (bf16[1,256,1536]{2,1,0:T(8,128)(2,1)S(1)}, bf16[1,256,1536]{2,1,0:T(8,128)(2,1)}, u32[]{:S(2)}) copy-start(bf16[1,256,1536]{2,1,0:T(8,128)(2,1)} %param.5) | copy-start | bytes 2359300
  20.0 33.7 %all-to-all-start = ((bf16[16,144,384]{2,1,0:T(8,128)(2,1)}), bf16[16,144,384]{2,1,0:T(8,128)(2,1)S(1)}, u32[]{:S(2)}, u32[]{:S(2)}) async-start(bf16[16,144,384]{2,1,0:T(8,128)(2,1)} %shard_map.78), calls=%async_computation | async-start | bytes 3538944 | tf_op jit(solution)/shard_map/all_to_all | solution.py:192
  27.7 10.1 %copy-start = (bf16[3,1536,384]{2,1,0:T(8,128)(2,1)S(1)}, bf16[3,1536,384]{2,1,0:T(8,128)(2,1)}, u32[]{:S(2)}) copy-start(bf16[3,1536,384]{2,1,0:T(8,128)(2,1)} %kernel_far.1) | copy-start | bytes 10616836
  30.6 7.2 %collective-permute-start.4 = (bf16[16,384]{1,0:T(8,128)(2,1)S(1)}, bf16[16,384]{1,0:T(8,128)(2,1)S(1)}, u32[]{:S(2)}, u32[]{:S(2)}) collective-permute-start(bf16[16,384]{1,0:T(8,128)(2,1)S(1)} %constant_dynamic-slice_fusion), channel_id=1, source_target_pairs={{4,8},{12,16},{20,24},{28,32},{36,40},{44,48},{52,56},{60,64},{68,... | collective-permute-start | bytes 36872 | tf_op jit(solution)/shard_map/ppermute | solution.py:18
  36.2 2.3 %copy-start.2 = (bf16[1,256,1536]{2,1,0:T(8,128)(2,1)S(1)}, bf16[1,256,1536]{2,1,0:T(8,128)(2,1)}, u32[]{:S(2)}) copy-start(bf16[1,256,1536]{2,1,0:T(8,128)(2,1)} %param.6) | copy-start | bytes 2359300
